TPU v7x, 256 devices: a whole 4x4x8 slice. The times are simulated.
256 devices in a mesh: head: 8 (over y, core), inner: 16 (over x_lo, z), outer: 2 (over x_hi).
Axes of the slice: x: 4 (x_hi: 2, x_lo: 2; x = x_hi * 2 + x_lo), y: 4, z: 8, core: 2. Of those that a mesh axis runs over, the one named last changes fastest.
Arguments:
- queries: bfloat16 [16384, 8192], P(('inner', 'outer', 'head')), may hold values from -12.816310409006173 to 12.816310409006173
- keys: bfloat16 [16384, 1024], P(('inner', 'outer', 'head')), may hold values from -4 to 4
- values: bfloat16 [16384, 1024], P(('inner', 'outer', 'head')), may hold values from -6 to 6
- dout: bfloat16 [16384, 8192], P(('inner', 'outer', 'head')), may hold values from -6 to 6
- doc_lengths: int32 [128], replicated, may hold values from 1 to 256, 16384 in all
- span_order: int32 [64], replicated, may hold values from 0 to 63, as said below
Outputs:
- attended: bfloat16 [16384, 8192], P(('inner', 'outer', 'head'))
- entropy: float32 [16384, 64], P(('inner', 'outer'), 'head')
- grad_query: bfloat16 [16384, 8192], P(('inner', 'outer', 'head'))
- grad_key: bfloat16 [16384, 1024], P(('inner', 'outer', 'head'))
- grad_value: bfloat16 [16384, 1024], P(('inner', 'outer', 'head'))
Inputs may be any that keep to these rules, and one draw needn't show every extreme that they name: `doc_lengths`: the 128 documents lie one after another over the 16384 positions of the sequence; the lengths sum to 16384 and the longest is exactly 256. Stored rows b * 256 to (b + 1) * 256 - 1 hold the sequence positions span_order[b] * 256 onward, in order; stored blocks 2 i and 2 i + 1 hold the spans i and 63 - i, in either order.
All inputs are finite; a program needn't handle non-finite values.
Results may differ from a plain program's by a relative error of at most 0.03.
Values may be sent and summed in bfloat16 or wider, within the bound.
A program may use at most 64 MiB of HBM per device.

v0:
```python
import math

import jax
import jax.numpy as jnp
from jax import lax
from jax.sharding import PartitionSpec as P

QUERY_HEADS = 64
KEY_VALUE_HEADS = 8
HEAD_WIDTH = 128


def shifted(value, axis, steps):
    count = lax.axis_size(axis)
    first, last = (max(0, -steps), min(count, count - steps))
    return lax.ppermute(value, axis, [(source, source + steps) for source in range(first, last)])


def doc_index(positions, doc_lengths):
    starts = jnp.cumsum(doc_lengths) - doc_lengths
    return jnp.sum((starts[None, :] <= positions[:, None]).astype(jnp.int32), axis=1) - 1


def linked(q_span, k_span, span_rows, doc_lengths):
    ends = doc_index(
        jnp.stack([k_span * span_rows + span_rows - 1, q_span * span_rows]), doc_lengths
    )
    return (k_span >= 0) & (ends[0] == ends[1])


def tile_scores(query_matrix_rows, key_matrix_rows, allowed):
    key_three = key_matrix_rows.reshape(
        key_matrix_rows.shape[0], query_matrix_rows.shape[1], HEAD_WIDTH
    )
    scores = jnp.einsum(
        "qhgd,thd->hgqt", query_matrix_rows, key_three, preferred_element_type=jnp.float32
    ) / math.sqrt(HEAD_WIDTH)
    return jnp.where(allowed, scores, -jnp.inf)


def blank_scores(query_matrix_rows, key_matrix_rows, allowed):
    return jnp.full(
        (
            query_matrix_rows.shape[1],
            query_matrix_rows.shape[2],
            query_matrix_rows.shape[0],
            key_matrix_rows.shape[0],
        ),
        -jnp.inf,
        jnp.float32,
    )


def forward_tile(scores, lse_rows, value_matrix_rows, allowed):
    probs = jnp.exp(scores - lse_rows[..., None])
    rounded_result = probs.astype(jnp.bfloat16)
    value_three = value_matrix_rows.reshape(
        value_matrix_rows.shape[0], lse_rows.shape[0], HEAD_WIDTH
    )
    mixed = jnp.einsum(
        "hgqt,thd->qhgd", rounded_result, value_three, preferred_element_type=jnp.float32
    )
    spread = jnp.sum(jnp.where(allowed, probs * scores, 0.0), axis=-1)
    return (rounded_result, mixed, spread)


def forward_blank(scores, lse_rows, value_matrix_rows, allowed):
    kv_count, group_count, row_count = lse_rows.shape
    mixed = jnp.zeros((row_count, kv_count, group_count, HEAD_WIDTH), jnp.float32)
    return (jnp.zeros(scores.shape, jnp.bfloat16), mixed, jnp.zeros_like(lse_rows))


def backward_tile(
    scores,
    lse_rows,
    delta_rows,
    key_matrix_rows,
    value_matrix_rows,
    output_gradient_rows,
    rounded_result,
    query_matrix_rows,
):
    kv_count = delta_rows.shape[0]
    key_three = key_matrix_rows.reshape(key_matrix_rows.shape[0], kv_count, HEAD_WIDTH)
    value_three = value_matrix_rows.reshape(value_matrix_rows.shape[0], kv_count, HEAD_WIDTH)
    probs = jnp.exp(scores - lse_rows[..., None])
    dprobs = jnp.einsum(
        "qhgd,thd->hgqt", output_gradient_rows, value_three, preferred_element_type=jnp.float32
    )
    score_gradient = (probs * (dprobs - delta_rows[..., None]) / math.sqrt(HEAD_WIDTH)).astype(
        jnp.bfloat16
    )
    dquery = jnp.einsum(
        "hgqt,thd->qhgd", score_gradient, key_three, preferred_element_type=jnp.float32
    )
    key_gradient = jnp.einsum(
        "ysfj,fysm->jym", score_gradient, query_matrix_rows, preferred_element_type=jnp.float32
    )
    value_gradient = jnp.einsum(
        "ysfj,fysm->jym", rounded_result, output_gradient_rows, preferred_element_type=jnp.float32
    )
    terms = jnp.concatenate(
        [
            key_gradient.reshape(key_gradient.shape[0], -1),
            value_gradient.reshape(value_gradient.shape[0], -1),
        ],
        axis=1,
    )
    return (dquery, terms)


def backward_blank(
    scores,
    lse_rows,
    delta_rows,
    key_matrix_rows,
    value_matrix_rows,
    output_gradient_rows,
    rounded_result,
    query_matrix_rows,
):
    terms = jnp.zeros((key_matrix_rows.shape[0], 2 * key_matrix_rows.shape[1]), jnp.float32)
    return (jnp.zeros(output_gradient_rows.shape, jnp.float32), terms)


def body(queries, keys, values, dout, doc_lengths, span_order):
    head_q, head_k, head_v, head_dout = (
        lax.all_to_all(queries, "head", split_axis=1, concat_axis=0, tiled=True),
        lax.all_to_all(keys, "head", split_axis=1, concat_axis=0, tiled=True),
        lax.all_to_all(values, "head", split_axis=1, concat_axis=0, tiled=True),
        lax.all_to_all(dout, "head", split_axis=1, concat_axis=0, tiled=True),
    )
    cycle_size = lax.axis_size(("inner", "outer"))
    own_index = lax.axis_index(("inner", "outer"))
    span_rows = head_q.shape[0] // 2
    kv_width = head_k.shape[1]
    kv_heads = kv_width // HEAD_WIDTH
    heads_per_group = QUERY_HEADS // KEY_VALUE_HEADS
    offsets = jnp.arange(span_rows, dtype=jnp.int32)
    is_top = own_index == cycle_size - 1
    slot_spans = [
        lax.dynamic_index_in_dim(span_order, 2 * own_index + slot_index, keepdims=False)
        for slot_index in range(2)
    ]
    slot_is_low = [slot_spans[slot_index] == own_index for slot_index in range(2)]
    first_low = slot_is_low[0]

    def slot_rows(source, slot_index):
        return source[slot_index * span_rows : (slot_index + 1) * span_rows]

    def lower_upper(source):
        return (
            jnp.where(first_low, slot_rows(source, 0), slot_rows(source, 1)),
            jnp.where(first_low, slot_rows(source, 1), slot_rows(source, 0)),
        )

    lower_keys, upper_keys = lower_upper(head_k)
    lower_values, upper_values = lower_upper(head_v)
    below_keys, below_values = shifted((lower_keys, lower_values), ("inner", "outer"), 1)
    above_keys, above_values = shifted((upper_keys, upper_values), ("inner", "outer"), -1)
    after_keys = jnp.where(is_top, lower_keys, above_keys)
    after_values = jnp.where(is_top, lower_values, above_values)

    def tile_mask(q_span, k_span, is_live):
        k_pos = k_span * span_rows + offsets
        q_pos = q_span * span_rows + offsets
        same_doc = doc_index(q_pos, doc_lengths)[:, None] == doc_index(k_pos, doc_lengths)[None, :]
        return same_doc & (k_pos[None, :] <= q_pos[:, None]) & is_live

    out_rows = []
    entropy_rows = []
    dquery_rows = []
    own_terms = []
    prev_terms = []
    for slot_index in range(2):
        q_span = slot_spans[slot_index]
        query_matrix_rows = slot_rows(head_q, slot_index).reshape(
            span_rows, kv_heads, heads_per_group, HEAD_WIDTH
        )
        output_gradient_rows = slot_rows(head_dout, slot_index).reshape(
            span_rows, kv_heads, heads_per_group, HEAD_WIDTH
        )
        own_keys = slot_rows(head_k, slot_index)
        own_values = slot_rows(head_v, slot_index)
        prev_keys = jnp.where(slot_is_low[slot_index], below_keys, after_keys)
        prev_values = jnp.where(slot_is_low[slot_index], below_values, after_values)
        prev_span = q_span - 1
        is_live = linked(q_span, prev_span, span_rows, doc_lengths)
        own_allowed = tile_mask(q_span, q_span, True)
        prev_allowed = tile_mask(q_span, jnp.maximum(prev_span, 0), is_live)
        own_scores = tile_scores(query_matrix_rows, own_keys, own_allowed)
        prev_scores = lax.cond(
            is_live, tile_scores, blank_scores, query_matrix_rows, prev_keys, prev_allowed
        )
        row_top = jnp.maximum(jnp.max(own_scores, axis=-1), jnp.max(prev_scores, axis=-1))
        row_total = jnp.sum(jnp.exp(own_scores - row_top[..., None]), axis=-1) + jnp.sum(
            jnp.exp(prev_scores - row_top[..., None]), axis=-1
        )
        lse_rows = row_top + jnp.log(row_total)
        own_rounded, own_mixed, own_spread = forward_tile(
            own_scores, lse_rows, own_values, own_allowed
        )
        prev_rounded, prev_mixed, prev_spread = lax.cond(
            is_live, forward_tile, forward_blank, prev_scores, lse_rows, prev_values, prev_allowed
        )
        out_tile = (own_mixed + prev_mixed).astype(jnp.bfloat16)
        out_rows.append(out_tile.reshape(span_rows, -1))
        entropy_rows.append(
            jnp.transpose(lse_rows - own_spread - prev_spread, (2, 0, 1)).reshape(
                span_rows, kv_heads * heads_per_group
            )
        )
        delta_rows = jnp.transpose(
            jnp.sum(
                output_gradient_rows.astype(jnp.float32) * out_tile.astype(jnp.float32), axis=-1
            ),
            (1, 2, 0),
        )
        own_dquery, own_grad = backward_tile(
            own_scores,
            lse_rows,
            delta_rows,
            own_keys,
            own_values,
            output_gradient_rows,
            own_rounded,
            query_matrix_rows,
        )
        prev_dquery, prev_grad = lax.cond(
            is_live,
            backward_tile,
            backward_blank,
            prev_scores,
            lse_rows,
            delta_rows,
            prev_keys,
            prev_values,
            output_gradient_rows,
            prev_rounded,
            query_matrix_rows,
        )
        dquery_rows.append((own_dquery + prev_dquery).astype(jnp.bfloat16).reshape(span_rows, -1))
        own_terms.append(own_grad)
        prev_terms.append(prev_grad)
    head_out = jnp.concatenate(out_rows, axis=0)
    entropy = jnp.concatenate(entropy_rows, axis=0)
    head_dq = jnp.concatenate(dquery_rows, axis=0)
    attended = lax.all_to_all(head_out, "head", split_axis=0, concat_axis=1, tiled=True)
    down_terms = jnp.where(first_low, prev_terms[0], prev_terms[1])
    upper_prev = jnp.where(first_low, prev_terms[1], prev_terms[0])
    zero_terms = jnp.zeros_like(upper_prev)
    send_upward = jnp.where(is_top, zero_terms, upper_prev)
    kept_local = jnp.where(is_top, upper_prev, zero_terms)
    from_upper = shifted(down_terms, ("inner", "outer"), -1)
    from_lower = shifted(send_upward, ("inner", "outer"), 1)
    grad_rows = []
    for slot_index in range(2):
        extra_terms = jnp.where(slot_is_low[slot_index], from_upper + kept_local, from_lower)
        grad_rows.append(own_terms[slot_index] + extra_terms)
    own_grads = jnp.concatenate(grad_rows, axis=0)
    head_dk = own_grads[:, :kv_width].astype(jnp.bfloat16)
    head_dv = own_grads[:, kv_width:].astype(jnp.bfloat16)
    grad_query, grad_key, grad_value = (
        lax.all_to_all(head_dq, "head", split_axis=0, concat_axis=1, tiled=True),
        lax.all_to_all(head_dk, "head", split_axis=0, concat_axis=1, tiled=True),
        lax.all_to_all(head_dv, "head", split_axis=0, concat_axis=1, tiled=True),
    )
    return (attended, entropy, grad_query, grad_key, grad_value)


def solution(mesh):
    placed = (
        P(("inner", "outer", "head"), None),
        P(("inner", "outer", "head"), None),
        P(("inner", "outer", "head"), None),
        P(("inner", "outer", "head"), None),
        P(),
        P(),
    )
    return jax.shard_map(
        body,
        mesh=mesh,
        in_specs=placed,
        out_specs=(
            P(("inner", "outer", "head"), None),
            P(("inner", "outer"), "head"),
            P(("inner", "outer", "head"), None),
            P(("inner", "outer", "head"), None),
            P(("inner", "outer", "head"), None),
        ),
        check_vma=False,
    )
```

profile of v0, /device:TPU:100, one launch (start us, length us, event | category | flops | bytes accessed | tf_op | source)
XLA Modules:
  0.0 251.8 jit_solution(9348624990498589816)
XLA Ops:
  2.2 4.5 %all-to-all-start = ((bf16[64,8,128]{2,0,1:T(8,128)(2,1)}), bf16[64,8,128]{2,0,1:T(8,128)(2,1)S(1)}, u32[]{:S(2)}, u32[]{:S(2)}) async-start(bf16[64,8,128]{2,0,1:T(8,128)(2,1)} %copy_bitcast_fusion.5), calls=%async_computation | async-start | bytes 262144 | tf_op jit(solution)/shard_map/all_to_all | solution.py:129
  24.1 4.8 %all-to-all-start.2 = ((bf16[64,8,128]{2,0,1:T(8,128)(2,1)}), bf16[64,8,128]{2,0,1:T(8,128)(2,1)S(1)}, u32[]{:S(2)}, u32[]{:S(2)}) async-start(bf16[64,8,128]{2,0,1:T(8,128)(2,1)} %copy_bitcast_fusion.4), calls=%async_computation.2 | async-start | bytes 262144 | tf_op jit(solution)/shard_map/all_to_all | solution.py:130
  29.0 5.0 %collective-permute-start = (bf16[256,128]{1,0:T(8,128)(2,1)S(1)}, bf16[256,128]{1,0:T(8,128)(2,1)S(1)}, u32[]{:S(2)}, u32[]{:S(2)}) collective-permute-start(bf16[256,128]{1,0:T(8,128)(2,1)S(1)} %get-tuple-element.282), channel_id=1, source_target_pairs={{0,1},{1,2},{2,3},{3,4},{4,5},{5,6},{6,7},{7,8},{8,9},{9,10},{10,1... | collective-permute-start | bytes 196616 | tf_op jit(solution)/shard_map/ppermute | solution.py:16
  36.3 4.8 %all-to-all-start.1 = ((bf16[64,8,1024]{2,0,1:T(8,128)(2,1)}), bf16[64,8,1024]{2,0,1:T(8,128)(2,1)S(1)}, u32[]{:S(2)}, u32[]{:S(2)}) async-start(bf16[64,8,1024]{2,0,1:T(8,128)(2,1)} %bitcast.406), calls=%async_computation.1 | async-start | bytes 2097152 | tf_op jit(solution)/shard_map/all_to_all | solution.py:128
  41.2 7.1 %collective-permute-start.2 = (bf16[256,128]{1,0:T(8,128)(2,1)S(1)}, bf16[256,128]{1,0:T(8,128)(2,1)S(1)}, u32[]{:S(2)}, u32[]{:S(2)}) collective-permute-start(bf16[256,128]{1,0:T(8,128)(2,1)S(1)} %get-tuple-element.278), channel_id=1, source_target_pairs={{0,1},{1,2},{2,3},{3,4},{4,5},{5,6},{6,7},{7,8},{8,9},{9,10},{10,1... | collective-permute-start | bytes 196616 | tf_op jit(solution)/shard_map/ppermute | solution.py:16
  50.9 7.2 %collective-permute-done.3 = bf16[256,128]{1,0:T(8,128)(2,1)S(1)} collective-permute-done((bf16[256,128]{1,0:T(8,128)(2,1)S(1)}, bf16[256,128]{1,0:T(8,128)(2,1)S(1)}, u32[]{:S(2)}, u32[]{:S(2)}) %collective-permute-start.3) | collective-permute-done | bytes 65568 | tf_op jit(solution)/shard_map/ppermute | solution.py:16
  58.7 4.8 %all-to-all-start.4 = ((bf16[64,8,1024]{2,0,1:T(8,128)(2,1)}), bf16[64,8,1024]{2,0,1:T(8,128)(2,1)}, u32[]{:S(2)}, u32[]{:S(2)}) async-start(bf16[64,8,1024]{2,0,1:T(8,128)(2,1)} %bitcast.405), calls=%async_computation.4 | async-start | bytes 2097152 | tf_op jit(solution)/shard_map/all_to_all | solution.py:131
  73.3 6.3 %all-to-all-done.4 = bf16[64,8,1024]{2,0,1:T(8,128)(2,1)} async-done(((bf16[64,8,1024]{2,0,1:T(8,128)(2,1)}), bf16[64,8,1024]{2,0,1:T(8,128)(2,1)}, u32[]{:S(2)}, u32[]{:S(2)}) %all-to-all-start.4) | async-done | bytes 1048608 | tf_op jit(solution)/shard_map/all_to_all | solution.py:131
  85.9 11.7 %conditional.7 = (bf16[1,8,256,256]{3,2,1,0:T(8,128)(2,1)}, f32[1,8,256]{2,1,0:T(8,128)}, f32[256,1,8,128]{0,3,2,1:T(8,128)}) conditional(s32[]{:T(128)} %convert_element_type.100, () %tuple.62, (f32[1,8,256]{2,1,0:T(8,128)S(1)}, f32[1,8,256,256]{2,3,1,0:T(8,128)}, bf16[256,128]{1,0:T(8,128)(2,1)}, pred[256,256]{1,0:T(8,128)(4,1)}) %tuple.159), branch_computations={%region_10.11_spmd, %region_11.13_spmd} | conditional | flops 136837120 | bytes 11943988 | solution.py:203
  88.9 3.7 %select_reduce_fusion = (f32[8,256]{1,0:T(8,128)}, bf16[1,8,256,256]{3,2,1,0:T(8,128)(2,1)}) fusion(f32[1,8,256,256]{3,2,1,0:T(8,128)} %copy.184, f32[8,256]{1,0:T(8,128)S(1)} %bitcast.443, pred[256,256]{1,0:T(8,128)(4,1)} %get-tuple-element.72), kind=kLoop, calls=%fused_computation.4 | loop fusion | flops 2619392 | bytes 3227648 | tf_op jit(solution)/shard_map/cond/branch_1_fun/reduce_sum | solution.py:63
  106.2 4.6 %conditional.8 = (f32[1,8,256,256]{2,3,1,0:T(8,128)S(1)}, f32[8,256]{1,0:T(8,128)}, f32[1,8,256]{2,1,0:T(8,128)S(1)}) conditional(s32[]{:T(128)} %convert_element_type.106, () %tuple.64, (pred[256,256]{1,0:T(8,128)(4,1)}, bf16[256,1,8,128]{3,2,0,1:T(8,128)(2,1)}, bf16[256,128]{1,0:T(8,128)(2,1)S(1)}) %tuple.156), branch_computations={%region_17.18_spmd, %region_18.20_spmd} | conditional | flops 135788544 | bytes 2908184 | solution.py:192
  122.8 11.8 %conditional.9 = (bf16[1,8,256,256]{3,2,1,0:T(8,128)(2,1)}, f32[1,8,256]{2,1,0:T(8,128)S(1)}, f32[256,1,8,128]{0,3,2,1:T(8,128)}) conditional(s32[]{:T(128)} %convert_element_type.106, () %tuple.66, (f32[1,8,256]{2,1,0:T(8,128)}, f32[1,8,256,256]{2,3,1,0:T(8,128)}, bf16[256,128]{1,0:T(8,128)(2,1)S(1)}, pred[256,256]{1,0:T(8,128)(4,1)S(1)}) %tuple.158), branch_computations={%region_22.23_spmd, %region_23.25_spmd} | conditional | flops 136837120 | bytes 11714612 | solution.py:203
  125.8 3.6 %select_reduce_fusion.1 = (f32[8,256]{1,0:T(8,128)}, bf16[1,8,256,256]{3,2,1,0:T(8,128)(2,1)}) fusion(f32[1,8,256,256]{3,2,1,0:T(8,128)} %copy.192, f32[8,256]{1,0:T(8,128)} %bitcast.445, pred[256,256]{1,0:T(8,128)(4,1)S(1)} %get-tuple-element.79), kind=kLoop, calls=%fused_computation.14 | loop fusion | flops 2619392 | bytes 3227648 | tf_op jit(solution)/shard_map/cond/branch_1_fun/reduce_sum | solution.py:63
  141.7 15.0 %conditional.10 = (f32[256,256]{0,1:T(8,128)S(1)}, f32[256,1,8,128]{0,3,2,1:T(8,128)}) conditional(s32[]{:T(128)} %convert_element_type.100, () %tuple.68, (f32[1,8,256]{2,1,0:T(8,128)S(1)}, f32[1,8,256,256]{2,3,1,0:T(8,128)S(1)}, bf16[256,1,8,128]{3,2,0,1:T(8,128)(2,1)S(1)}, bf16[256,128]{1,0:T(8,128)(2,1)S(1)}, f32[1,8,256]{2,1,0:T(8,128)S(1)}, ...), branch_computations={%region_28.29_spmd, %region_29.30_spmd} | conditional | flops 539557888 | bytes 18235436 | solution.py:229
  156.6 12.3 %conditional.11 = (f32[256,256]{0,1:T(8,128)}, f32[256,1,8,128]{0,3,2,1:T(8,128)}) conditional(s32[]{:T(128)} %convert_element_type.106, () %tuple.70, (f32[1,8,256]{2,1,0:T(8,128)}, f32[1,8,256,256]{2,3,1,0:T(8,128)}, bf16[256,1,8,128]{3,2,0,1:T(8,128)(2,1)S(1)}, bf16[256,128]{1,0:T(8,128)(2,1)}, f32[1,8,256]{2,1,0:T(8,128)}, ...), branch_computations={%region_31.32_spmd, %region_32.33_spmd} | conditional | flops 539557888 | bytes 18497608 | solution.py:229
  171.9 7.5 %collective-permute-start.5 = (f32[256,256]{0,1:T(8,128)S(1)}, f32[256,256]{0,1:T(8,128)S(1)}, u32[]{:S(2)}, u32[]{:S(2)}) collective-permute-start(f32[256,256]{0,1:T(8,128)S(1)} %get-tuple-element.270), channel_id=1, source_target_pairs={{0,1},{1,2},{2,3},{3,4},{4,5},{5,6},{6,7},{7,8},{8,9},{9,10},{10,1... | collective-permute-start | bytes 786440 | tf_op jit(solution)/shard_map/ppermute | solution.py:16
  183.3 5.3 %collective-permute-done.5 = f32[256,256]{0,1:T(8,128)S(1)} collective-permute-done((f32[256,256]{0,1:T(8,128)S(1)}, f32[256,256]{0,1:T(8,128)S(1)}, u32[]{:S(2)}, u32[]{:S(2)}) %collective-permute-start.5) | collective-permute-done | bytes 262176 | tf_op jit(solution)/shard_map/ppermute | solution.py:16
  191.2 3.6 %all-to-all-start.7 = ((bf16[8,64,128]{2,1,0:T(8,128)(2,1)}), bf16[8,64,128]{2,1,0:T(8,128)(2,1)S(1)}, u32[]{:S(2)}, u32[]{:S(2)}) async-start(bf16[8,64,128]{2,1,0:T(8,128)(2,1)} %bitcast.441), calls=%async_computation.7 | async-start | bytes 262144 | tf_op jit(solution)/shard_map/all_to_all | solution.py:266
  201.1 4.5 %all-to-all-start.6 = ((bf16[8,64,128]{2,1,0:T(8,128)(2,1)}), bf16[8,64,128]{2,1,0:T(8,128)(2,1)}, u32[]{:S(2)}, u32[]{:S(2)}) async-start(bf16[8,64,128]{2,1,0:T(8,128)(2,1)} %bitcast.442), calls=%async_computation.6 | async-start | bytes 262144 | tf_op jit(solution)/shard_map/all_to_all | solution.py:265
  206.7 5.2 %all-to-all-done.6 = bf16[8,64,128]{2,1,0:T(8,128)(2,1)} async-done(((bf16[8,64,128]{2,1,0:T(8,128)(2,1)}), bf16[8,64,128]{2,1,0:T(8,128)(2,1)}, u32[]{:S(2)}, u32[]{:S(2)}) %all-to-all-start.6) | async-done | bytes 131104 | tf_op jit(solution)/shard_map/all_to_all | solution.py:265
  211.8 3.6 %all-to-all-start.5 = ((bf16[8,64,1024]{2,1,0:T(8,128)(2,1)}), bf16[8,64,1024]{2,1,0:T(8,128)(2,1)S(1)}, u32[]{:S(2)}, u32[]{:S(2)}) async-start(bf16[8,64,1024]{2,1,0:T(8,128)(2,1)} %bitcast.417), calls=%async_computation.5 | async-start | bytes 2097152 | tf_op jit(solution)/shard_map/all_to_all | solution.py:264
  222.9 8.4 %all-to-all-done.5 = bf16[8,64,1024]{2,1,0:T(8,128)(2,1)S(1)} async-done(((bf16[8,64,1024]{2,1,0:T(8,128)(2,1)}), bf16[8,64,1024]{2,1,0:T(8,128)(2,1)S(1)}, u32[]{:S(2)}, u32[]{:S(2)}) %all-to-all-start.5) | async-done | bytes 1048608 | tf_op jit(solution)/shard_map/all_to_all | solution.py:264
  231.3 3.6 %all-to-all-start.3 = ((bf16[8,64,1024]{2,1,0:T(8,128)(2,1)}), bf16[8,64,1024]{2,1,0:T(8,128)(2,1)S(1)}, u32[]{:S(2)}, u32[]{:S(2)}) async-start(bf16[8,64,1024]{2,1,0:T(8,128)(2,1)} %bitcast.100), calls=%async_computation.3 | async-start | bytes 2097152 | tf_op jit(solution)/shard_map/all_to_all | solution.py:248
  239.5 11.2 %all-to-all-done.3 = bf16[8,64,1024]{2,1,0:T(8,128)(2,1)S(1)} async-done(((bf16[8,64,1024]{2,1,0:T(8,128)(2,1)}), bf16[8,64,1024]{2,1,0:T(8,128)(2,1)S(1)}, u32[]{:S(2)}, u32[]{:S(2)}) %all-to-all-start.3) | async-done | bytes 1048608 | tf_op jit(solution)/shard_map/all_to_all | solution.py:248
  (230 shorter events, 142.4 us)
Async XLA Ops:
  0.6 18.3 %copy-start.42 = (bf16[64,1024]{1,0:T(8,128)(2,1)S(1)}, bf16[64,1024]{1,0:T(8,128)(2,1)}, u32[]{:S(2)}) copy-start(bf16[64,1024]{1,0:T(8,128)(2,1)} %param.20) | copy-start | bytes 393220
  1.5 18.1 %copy-start.21 = (bf16[64,8192]{1,0:T(8,128)(2,1)S(1)}, bf16[64,8192]{1,0:T(8,128)(2,1)}, u32[]{:S(2)}) copy-start(bf16[64,8192]{1,0:T(8,128)(2,1)} %param.21) | copy-start | bytes 3145732
  2.2 21.9 %all-to-all-start = ((bf16[64,8,128]{2,0,1:T(8,128)(2,1)}), bf16[64,8,128]{2,0,1:T(8,128)(2,1)S(1)}, u32[]{:S(2)}, u32[]{:S(2)}) async-start(bf16[64,8,128]{2,0,1:T(8,128)(2,1)} %copy_bitcast_fusion.5), calls=%async_computation | async-start | bytes 262144 | tf_op jit(solution)/shard_map/all_to_all | solution.py:129
  18.8 47.9 %copy-start.33 = (pred[256,256]{1,0:T(8,128)(4,1)}, pred[256,256]{1,0:T(8,128)(4,1)S(1)}, u32[]{:S(2)}) copy-start(pred[256,256]{1,0:T(8,128)(4,1)S(1)} %get-tuple-element.285) | copy-start | bytes 196612
  19.0 52.1 %copy-start.28 = (pred[256,256]{0,1:T(8,128)(4,1)}, pred[256,256]{0,1:T(8,128)(4,1)S(1)}, u32[]{:S(2)}) copy-start(pred[256,256]{0,1:T(8,128)(4,1)S(1)} %copy.175) | copy-start | bytes 196612
  24.1 12.2 %all-to-all-start.2 = ((bf16[64,8,128]{2,0,1:T(8,128)(2,1)}), bf16[64,8,128]{2,0,1:T(8,128)(2,1)S(1)}, u32[]{:S(2)}, u32[]{:S(2)}) async-start(bf16[64,8,128]{2,0,1:T(8,128)(2,1)} %copy_bitcast_fusion.4), calls=%async_computation.2 | async-start | bytes 262144 | tf_op jit(solution)/shard_map/all_to_all | solution.py:130
  29.0 21.3 %collective-permute-start = (bf16[256,128]{1,0:T(8,128)(2,1)S(1)}, bf16[256,128]{1,0:T(8,128)(2,1)S(1)}, u32[]{:S(2)}, u32[]{:S(2)}) collective-permute-start(bf16[256,128]{1,0:T(8,128)(2,1)S(1)} %get-tuple-element.282), channel_id=1, source_target_pairs={{0,1},{1,2},{2,3},{3,4},{4,5},{5,6},{6,7},{7,8},{8,9},{9,10},{10,1... | collective-permute-start | bytes 196616 | tf_op jit(solution)/shard_map/ppermute | solution.py:16
  34.0 16.3 %collective-permute-start.1 = (bf16[256,128]{1,0:T(8,128)(2,1)S(1)}, bf16[256,128]{1,0:T(8,128)(2,1)S(1)}, u32[]{:S(2)}, u32[]{:S(2)}) collective-permute-start(bf16[256,128]{1,0:T(8,128)(2,1)S(1)} %get-tuple-element.281), channel_id=1, source_target_pairs={{1,0},{2,1},{3,2},{4,3},{5,4},{6,5},{7,6},{8,7},{9,8},{10,9},{11,1... | collective-permute-start | bytes 196616 | tf_op jit(solution)/shard_map/ppermute | solution.py:16
  36.3 22.4 %all-to-all-start.1 = ((bf16[64,8,1024]{2,0,1:T(8,128)(2,1)}), bf16[64,8,1024]{2,0,1:T(8,128)(2,1)S(1)}, u32[]{:S(2)}, u32[]{:S(2)}) async-start(bf16[64,8,1024]{2,0,1:T(8,128)(2,1)} %bitcast.406), calls=%async_computation.1 | async-start | bytes 2097152 | tf_op jit(solution)/shard_map/all_to_all | solution.py:128
  41.2 9.7 %collective-permute-start.2 = (bf16[256,128]{1,0:T(8,128)(2,1)S(1)}, bf16[256,128]{1,0:T(8,128)(2,1)S(1)}, u32[]{:S(2)}, u32[]{:S(2)}) collective-permute-start(bf16[256,128]{1,0:T(8,128)(2,1)S(1)} %get-tuple-element.278), channel_id=1, source_target_pairs={{0,1},{1,2},{2,3},{3,4},{4,5},{5,6},{6,7},{7,8},{8,9},{9,10},{10,1... | collective-permute-start | bytes 196616 | tf_op jit(solution)/shard_map/ppermute | solution.py:16
  48.3 9.8 %collective-permute-start.3 = (bf16[256,128]{1,0:T(8,128)(2,1)S(1)}, bf16[256,128]{1,0:T(8,128)(2,1)S(1)}, u32[]{:S(2)}, u32[]{:S(2)}) collective-permute-start(bf16[256,128]{1,0:T(8,128)(2,1)S(1)} %get-tuple-element.277), channel_id=1, source_target_pairs={{1,0},{2,1},{3,2},{4,3},{5,4},{6,5},{7,6},{8,7},{9,8},{10,9},{11,1... | collective-permute-start | bytes 196616 | tf_op jit(solution)/shard_map/ppermute | solution.py:16
  50.9 15.8 %copy-start.27 = (bf16[256,128]{1,0:T(8,128)(2,1)}, bf16[256,128]{1,0:T(8,128)(2,1)S(1)}, u32[]{:S(2)}) copy-start(bf16[256,128]{1,0:T(8,128)(2,1)S(1)} %get-tuple-element.275) | copy-start | bytes 196612
  58.7 20.8 %all-to-all-start.4 = ((bf16[64,8,1024]{2,0,1:T(8,128)(2,1)}), bf16[64,8,1024]{2,0,1:T(8,128)(2,1)}, u32[]{:S(2)}, u32[]{:S(2)}) async-start(bf16[64,8,1024]{2,0,1:T(8,128)(2,1)} %bitcast.405), calls=%async_computation.4 | async-start | bytes 2097152 | tf_op jit(solution)/shard_map/all_to_all | solution.py:131
  168.9 19.7 %copy-start.34 = (f32[256,128]{0,1:T(8,128)S(1)}, f32[256,128]{0,1:T(8,128)}, u32[]{:S(2)}) copy-start(f32[256,128]{0,1:T(8,128)} %convolution_bitcast_fusion.15) | copy-start | bytes 393220
  168.9 19.7 %copy-start.36 = (f32[256,128]{0,1:T(8,128)S(1)}, f32[256,128]{0,1:T(8,128)}, u32[]{:S(2)}) copy-start(f32[256,128]{0,1:T(8,128)} %convolution_bitcast_fusion.14) | copy-start | bytes 393220
  169.9 13.4 %collective-permute-start.4 = (f32[256,256]{0,1:T(8,128)S(1)}, f32[256,256]{0,1:T(8,128)S(1)}, u32[]{:S(2)}, u32[]{:S(2)}) collective-permute-start(f32[256,256]{0,1:T(8,128)S(1)} %get-tuple-element.269), channel_id=1, source_target_pairs={{1,0},{2,1},{3,2},{4,3},{5,4},{6,5},{7,6},{8,7},{9,8},{10,9},{11,1... | collective-permute-start | bytes 786440 | tf_op jit(solution)/shard_map/ppermute | solution.py:16
  171.9 16.8 %collective-permute-start.5 = (f32[256,256]{0,1:T(8,128)S(1)}, f32[256,256]{0,1:T(8,128)S(1)}, u32[]{:S(2)}, u32[]{:S(2)}) collective-permute-start(f32[256,256]{0,1:T(8,128)S(1)} %get-tuple-element.270), channel_id=1, source_target_pairs={{0,1},{1,2},{2,3},{3,4},{4,5},{5,6},{6,7},{7,8},{8,9},{9,10},{10,1... | collective-permute-start | bytes 786440 | tf_op jit(solution)/shard_map/ppermute | solution.py:16
  181.9 12.9 %copy-start.18 = (f32[256,1,8,128]{0,3,2,1:T(8,128)S(1)}, f32[256,1,8,128]{0,3,2,1:T(8,128)}, u32[]{:S(2)}) copy-start(f32[256,1,8,128]{0,3,2,1:T(8,128)} %convolution_bitcast_fusion.8) | copy-start | bytes 3145732
  191.2 9.9 %all-to-all-start.7 = ((bf16[8,64,128]{2,1,0:T(8,128)(2,1)}), bf16[8,64,128]{2,1,0:T(8,128)(2,1)S(1)}, u32[]{:S(2)}, u32[]{:S(2)}) async-start(bf16[8,64,128]{2,1,0:T(8,128)(2,1)} %bitcast.441), calls=%async_computation.7 | async-start | bytes 262144 | tf_op jit(solution)/shard_map/all_to_all | solution.py:266
  201.1 10.7 %all-to-all-start.6 = ((bf16[8,64,128]{2,1,0:T(8,128)(2,1)}), bf16[8,64,128]{2,1,0:T(8,128)(2,1)}, u32[]{:S(2)}, u32[]{:S(2)}) async-start(bf16[8,64,128]{2,1,0:T(8,128)(2,1)} %bitcast.442), calls=%async_computation.6 | async-start | bytes 262144 | tf_op jit(solution)/shard_map/all_to_all | solution.py:265
  211.8 19.4 %all-to-all-start.5 = ((bf16[8,64,1024]{2,1,0:T(8,128)(2,1)}), bf16[8,64,1024]{2,1,0:T(8,128)(2,1)S(1)}, u32[]{:S(2)}, u32[]{:S(2)}) async-start(bf16[8,64,1024]{2,1,0:T(8,128)(2,1)} %bitcast.417), calls=%async_computation.5 | async-start | bytes 2097152 | tf_op jit(solution)/shard_map/all_to_all | solution.py:264
  222.4 13.1 %copy-start.41 = (f32[1,8,256]{2,1,0:T(8,128)S(1)}, f32[1,8,256]{2,1,0:T(8,128)}, u32[]{:S(2)}) copy-start(f32[1,8,256]{2,1,0:T(8,128)} %bitcast_add_fusion) | copy-start | bytes 24580
  222.4 13.1 %copy-start.49 = (f32[1,8,256]{2,1,0:T(8,128)S(1)}, f32[1,8,256]{2,1,0:T(8,128)}, u32[]{:S(2)}) copy-start(f32[1,8,256]{2,1,0:T(8,128)} %copy-done.48) | copy-start | bytes 24580
  231.3 19.4 %all-to-all-start.3 = ((bf16[8,64,1024]{2,1,0:T(8,128)(2,1)}), bf16[8,64,1024]{2,1,0:T(8,128)(2,1)S(1)}, u32[]{:S(2)}, u32[]{:S(2)}) async-start(bf16[8,64,1024]{2,1,0:T(8,128)(2,1)} %bitcast.100), calls=%async_computation.3 | async-start | bytes 2097152 | tf_op jit(solution)/shard_map/all_to_all | solution.py:248
  (40 other events, 141.0 us)
where the time goes:
time: 254 us; the launch traced here: 252 us
  local copies, waits for them, and re-layouts  63.3 us (25%)
  starting transfers between devices  59.9 us (24%)
  waiting for transfers between devices  44.9 us (18%)
  matrix products  39.2 us (15%)
  other arithmetic  36.6 us (14%)
  between operations  7.64 us (3%)
    ppermute x6, starting transfers between devices, shifted(): lax.ppermute(value, axis, [(source, source + steps) for source in range(f...  25.8 us
    another operation x13, local copies, waits for them, and re-layouts  17.5 us
    ppermute x6, waiting for transfers between devices, shifted(): lax.ppermute(value, axis, [(source, source + steps) for source in range(f...  13.9 us
    all_to_all x1, waiting for transfers between devices, body(): lax.all_to_all(head_out, 'head', split_axis=0, concat_axis=1, tiled=True)  11.2 us
    dot_general x4, matrix products, forward_tile(): jnp.einsum('hgqt,thd->qhgd', rounded_result, value_three, preferred_eleme...  9.94 us
    all_to_all x1, waiting for transfers between devices, body(): lax.all_to_all(head_dq, 'head', split_axis=0, concat_axis=1, tiled=True)  8.37 us
    reduce_sum x4, other arithmetic, forward_tile(): spread = jnp.sum(jnp.where(allowed, probs * scores, 0.0), axis=-1)  8.19 us
    unnamed x94, local copies, waits for them, and re-layouts  7.76 us
  transfers between devices with their start and end apart: 14, of which 7 were waited for; matrix products, arithmetic and copies ran while one was open for 17% of the time, Pallas kernels for 0%

commit v1 on v0

v1 whole, which is shorter than its diff:
```python
import functools
import math

import jax
import jax.numpy as jnp
from jax import lax
from jax.experimental import pallas as pl
from jax.experimental.pallas import tpu as pltpu
from jax.sharding import PartitionSpec as P

MESH = pl.DeviceIdType.MESH
F32 = jnp.float32
BF16 = jnp.bfloat16
NEG = -1.0e30
LN2 = math.log(2.0)

D = 128
HEADS = 8
ROWS = 64
SPAN = 256
KEYS = 320
STEPS = SPAN // ROWS


def place():
    me = lax.axis_index("head")
    outer_size = lax.axis_size("outer")
    cycle = lax.axis_size("inner") * outer_size
    own = lax.axis_index("inner") * outer_size + lax.axis_index("outer")

    def at(index):
        return {"inner": index // outer_size, "outer": lax.rem(index, outer_size)}

    above = at(lax.rem(own + 1, cycle))
    below = at(lax.rem(own + cycle - 1, cycle))
    return me, me // STEPS, lax.rem(me, STEPS), own, cycle, above, below


def greet(me, above, below):
    barrier = pltpu.get_barrier_semaphore()
    for step in range(1, HEADS):
        pl.semaphore_signal(
            barrier, inc=1, device_id={"head": lax.rem(me + step, HEADS)}, device_id_type=MESH
        )
    pl.semaphore_signal(barrier, inc=1, device_id=above, device_id_type=MESH)
    pl.semaphore_signal(barrier, inc=1, device_id=below, device_id_type=MESH)
    pl.semaphore_wait(barrier, HEADS + 1)


def remote(src, dst, send, recv, device):
    return pltpu.make_async_remote_copy(
        src_ref=src, dst_ref=dst, send_sem=send, recv_sem=recv, device_id=device, device_id_type=MESH
    )


def gather_kernel(
    order_ref, k_ref, v_ref, kk_ref, vv_ref,
    hb, nb, rb, sel,
    s1_send, s1_recv, own_send, own_recv, s2_send, s2_recv, s3_send, s3_recv, local,
):
    me, half, j, own, cycle, above, below = place()
    ins, outs = (k_ref, v_ref), (kk_ref, vv_ref)
    first_low = order_ref[2 * own] == own
    greet(me, above, below)

    def spread(p, kv, src):
        return remote(
            ins[kv].at[:, pl.ds(p * D, D)], hb.at[kv, pl.ds(src * ROWS, ROWS)],
            s1_send.at[p, kv], s1_recv.at[src, kv], {"head": p},
        )

    for p in range(HEADS):
        @pl.when(me != p)
        def _(p=p):
            for kv in range(2):
                spread(p, kv, me).start()

    own_rows = pl.ds(SPAN + j * ROWS, ROWS)
    mine = [
        pltpu.make_async_copy(
            ins[kv].at[:, pl.ds(me * D, D)], hb.at[kv, pl.ds(me * ROWS, ROWS)], local.at[kv]
        )
        for kv in range(2)
    ] + [
        pltpu.make_async_copy(ins[kv], outs[kv].at[own_rows], local.at[2 + kv]) for kv in range(2)
    ]
    for copy in mine:
        copy.start()
    for copy in mine:
        copy.wait()
    for p in range(HEADS):
        @pl.when(me != p)
        def _(p=p):
            for kv in range(2):
                spread(p, kv, p).wait_recv()

    a, b = hb[:, :SPAN], hb[:, SPAN:]
    nb[0] = jnp.where(first_low, a, b)
    nb[1] = jnp.where(first_low, b, a)
    low = remote(nb.at[0], rb.at[0], s2_send.at[0], s2_recv.at[0], above)
    high = remote(nb.at[1], rb.at[1], s2_send.at[1], s2_recv.at[1], below)
    low.start()
    high.start()

    def share(jj, kv, src):
        return remote(
            ins[kv], outs[kv].at[pl.ds(SPAN + src * ROWS, ROWS)],
            own_send.at[jj, kv], own_recv.at[src, kv], {"head": half * STEPS + jj},
        )

    for jj in range(1, STEPS):
        @pl.when(j < jj)
        def _(jj=jj):
            for kv in range(2):
                share(jj, kv, j).start()

    low.wait_recv()
    high.wait_recv()
    prev_low = rb[0]
    prev_high = jnp.where(own == cycle - 1, nb[0], rb[1])
    sel[0] = jnp.where(first_low, prev_low, prev_high)
    sel[1] = jnp.where(first_low, prev_high, prev_low)

    def deliver(p, kv, src, jj):
        rows = pl.ds(jj * ROWS, SPAN - jj * ROWS)
        return remote(
            sel.at[p // STEPS, kv, rows], outs[kv].at[rows, pl.ds(src * D, D)],
            s3_send.at[p, kv], s3_recv.at[src, kv], {"head": p},
        )

    for p in range(HEADS):
        @pl.when(me != p)
        def _(p=p):
            for kv in range(2):
                deliver(p, kv, me, p % STEPS).start()

    back = [
        pltpu.make_async_copy(
            sel.at[half, kv], outs[kv].at[pl.ds(0, SPAN), pl.ds(me * D, D)], local.at[kv]
        )
        for kv in range(2)
    ]
    for copy in back:
        copy.start()
    for jj in range(STEPS):
        @pl.when(j == jj)
        def _(jj=jj):
            for p in range(HEADS):
                @pl.when(me != p)
                def _(p=p):
                    for kv in range(2):
                        deliver(p, kv, p, jj).wait_recv()
    for jj in range(STEPS - 1):
        @pl.when(jj < j)
        def _(jj=jj):
            for kv in range(2):
                share(0, kv, jj).wait_recv()
    for copy in back:
        copy.wait()
    for p in range(HEADS):
        @pl.when(me != p)
        def _(p=p):
            for kv in range(2):
                spread(p, kv, me).wait_send()
                deliver(p, kv, me, p % STEPS).wait_send()
    for jj in range(1, STEPS):
        @pl.when(j < jj)
        def _(jj=jj):
            for kv in range(2):
                share(jj, kv, j).wait_send()
    low.wait_send()
    high.wait_send()


def attend_kernel(
    order_ref, len_ref, q_ref, do_ref, k_ref, v_ref,
    out_ref, dq_ref, gk_ref, gv_ref, ok_ref, ov_ref, ent_ref,
    bias_ref,
):
    me, half, j, own, cycle, above, below = place()
    rows = pl.multiple_of(j * ROWS, ROWS)

    @pl.when(pl.program_id(0) == 0)
    def _():
        start_pos = order_ref[2 * own + half] * SPAN + j * ROWS
        lens = jnp.broadcast_to(len_ref[...], (D, D)).astype(F32)
        row = lax.broadcasted_iota(jnp.int32, (D, D), 0)
        col = lax.broadcasted_iota(jnp.int32, (D, D), 1)
        starts = jnp.sum(jnp.where(col < row, lens, 0.0), axis=1, keepdims=True)
        lane = lax.broadcasted_iota(jnp.int32, (D, D), 1) % ROWS
        pos = (start_pos + lane).astype(F32)
        found = jnp.max(jnp.where(starts <= pos, starts, 0.0), axis=0, keepdims=True)
        first = found.astype(jnp.int32) - (start_pos - SPAN)
        key = lax.broadcasted_iota(jnp.int32, (KEYS, D), 0)
        query = lax.broadcasted_iota(jnp.int32, (KEYS, D), 1) % ROWS
        allowed = (key >= first) & (key <= query + SPAN)
        bias_ref[...] = jnp.where(allowed, 0.0, NEG)

    k5 = k_ref[pl.ds(rows, KEYS), :]
    v5 = v_ref[pl.ds(rows, KEYS), :]
    k5t, v5t = k5.T, v5.T
    scale = 1.0 / math.sqrt(D)
    nt = (((1,), (1,)), ((), ()))
    nn = (((1,), (0,)), ((), ()))
    per = 4
    lanes = per * ROWS
    bias = jnp.concatenate([bias_ref[...]] * (lanes // D), axis=1)
    sub = lax.broadcasted_iota(jnp.int32, (HEADS, D), 0)
    ent = jnp.zeros((HEADS, D), F32)
    dk = jnp.zeros((KEYS, D), F32)
    dv = jnp.zeros((KEYS, D), F32)
    for chunk in range(HEADS // per):
        heads = range(chunk * per, (chunk + 1) * per)
        q = jnp.concatenate([q_ref[:, g * D : (g + 1) * D] for g in heads], axis=0)
        do = jnp.concatenate([do_ref[:, g * D : (g + 1) * D] for g in heads], axis=0)
        t = lax.dot_general(k5, q, nt, preferred_element_type=F32) * (scale / LN2) + bias
        dp = lax.dot_general(v5, do, nt, preferred_element_type=F32)
        u = t - jnp.max(t, axis=0, keepdims=True)
        e = jnp.exp2(u)
        total = jnp.sum(e, axis=0, keepdims=True)
        inv = 1.0 / total
        p = e * inv
        spread = jnp.sum(p * u, axis=0, keepdims=True)
        entropy = LN2 * (jnp.log2(total) - spread)
        pb = p.astype(BF16)
        delta = jnp.sum(p * dp, axis=0, keepdims=True)
        ds = (p * ((dp - delta) * scale)).astype(BF16)
        out = lax.dot_general(v5t, pb, nn, preferred_element_type=F32)
        dq = lax.dot_general(k5t, ds, nn, preferred_element_type=F32)
        dv = dv + lax.dot_general(pb, do, nn, preferred_element_type=F32)
        dk = dk + lax.dot_general(ds, q, nn, preferred_element_type=F32)
        out_t, dq_t = out.T.astype(BF16), dq.T.astype(BF16)
        for n, g in enumerate(heads):
            out_ref[:, g * D : (g + 1) * D] = out_t[n * ROWS : (n + 1) * ROWS]
            dq_ref[:, g * D : (g + 1) * D] = dq_t[n * ROWS : (n + 1) * ROWS]
        for n in range(per // 2):
            pair = jnp.broadcast_to(entropy[:, n * D : (n + 1) * D], (HEADS, D))
            g = chunk * per + 2 * n
            ent = jnp.where(sub == g, pair, ent)
            ent = jnp.where(sub == g + 1, pltpu.roll(pair, ROWS, 1), ent)
    ent_ref[0] = ent
    gk_ref[pl.ds(rows, SPAN), :] = dk[:SPAN].astype(BF16)
    gv_ref[pl.ds(rows, SPAN), :] = dv[:SPAN].astype(BF16)
    ok_ref[...] = dk[SPAN:]
    ov_ref[...] = dv[SPAN:]


def scatter_kernel(
    order_ref, gk_ref, gv_ref, ok_ref, ov_ref, ent_ref, dk_ref, dv_ref, ent_out,
    cb, nb, rb, sb, xb, ob, eb,
    s3_send, s3_recv, own_send, own_recv, s2_send, s2_recv, s1_send, s1_recv, e_send, e_recv, local,
):
    me, half, j, own, cycle, above, below = place()
    grads, owns, outs = (gk_ref, gv_ref), (ok_ref, ov_ref), (dk_ref, dv_ref)
    first_low = order_ref[2 * own] == own
    greet(me, above, below)

    def collect(p, kv, src, jj):
        rows = pl.ds(jj * ROWS, SPAN - jj * ROWS)
        return remote(
            grads[kv].at[rows, pl.ds(p * D, D)], cb.at[src, kv, rows],
            s3_send.at[p, kv], s3_recv.at[src, kv], {"head": p},
        )

    def share(jj, kv, src):
        return remote(
            grads[kv].at[pl.ds(SPAN + jj * ROWS, ROWS)], ob.at[src, kv],
            own_send.at[jj, kv], own_recv.at[src, kv], {"head": half * STEPS + jj},
        )

    def entropy(p, src):
        return remote(ent_ref.at[p], eb.at[src], e_send.at[p], e_recv.at[src], {"head": p})

    mine = [
        pltpu.make_async_copy(
            grads[kv].at[pl.ds(0, SPAN), pl.ds(me * D, D)], cb.at[me, kv], local.at[kv]
        )
        for kv in range(2)
    ] + [pltpu.make_async_copy(ent_ref.at[me], eb.at[me], local.at[2])]
    for jj in range(STEPS):
        @pl.when(j == jj)
        def _(jj=jj):
            for p in range(HEADS):
                @pl.when(me != p)
                def _(p=p):
                    for kv in range(2):
                        collect(p, kv, me, jj).start()
    for copy in mine:
        copy.start()
    for copy in mine:
        copy.wait()
    for p in range(HEADS):
        @pl.when(me != p)
        def _(p=p):
            for kv in range(2):
                collect(p, kv, p, p % STEPS).wait_recv()

    def summed(side):
        blocks = []
        for b in range(STEPS):
            rows = slice(b * ROWS, (b + 1) * ROWS)
            total = cb[side * STEPS, :, rows].astype(F32)
            for jj in range(1, b + 1):
                total = total + cb[side * STEPS + jj, :, rows].astype(F32)
            blocks.append(total.astype(BF16))
        return jnp.concatenate(blocks, axis=1)

    a, b = summed(0), summed(1)
    nb[0] = jnp.where(first_low, a, b)
    nb[1] = jnp.where(first_low, b, a)
    low = remote(nb.at[0], rb.at[0], s2_send.at[0], s2_recv.at[0], below)
    high = remote(nb.at[1], rb.at[1], s2_send.at[1], s2_recv.at[1], above)
    low.start()
    high.start()
    for jj in range(STEPS - 1):
        @pl.when(jj < j)
        def _(jj=jj):
            for kv in range(2):
                share(jj, kv, j).start()
    for p in range(HEADS):
        @pl.when(me != p)
        def _(p=p):
            entropy(p, me).start()
    low.wait_recv()
    high.wait_recv()
    low_part = jnp.where(own == cycle - 1, nb[1], rb[0])
    high_part = jnp.where(own == 0, jnp.zeros_like(rb[1]), rb[1])
    sb[0] = jnp.where(first_low, low_part, high_part)
    sb[1] = jnp.where(first_low, high_part, low_part)

    def deliver(p, kv, src):
        return remote(
            sb.at[p // STEPS, kv, pl.ds((p % STEPS) * ROWS, ROWS)], xb.at[kv, :, pl.ds(src * D, D)],
            s1_send.at[p, kv], s1_recv.at[src, kv], {"head": p},
        )

    for p in range(HEADS):
        @pl.when(me != p)
        def _(p=p):
            for kv in range(2):
                deliver(p, kv, me).start()
    back = [
        pltpu.make_async_copy(
            sb.at[half, kv, pl.ds(j * ROWS, ROWS)], xb.at[kv, :, pl.ds(me * D, D)], local.at[kv]
        )
        for kv in range(2)
    ]
    for copy in back:
        copy.start()
    for p in range(HEADS):
        @pl.when(me != p)
        def _(p=p):
            entropy(p, p).wait_recv()
    for n in range(HEADS // 2):
        ent_out[:, n * D : n * D + ROWS] = eb[2 * n, :, :ROWS]
        ent_out[:, n * D + ROWS : (n + 1) * D] = eb[2 * n + 1, :, :ROWS]
    ob[0] = jnp.zeros_like(ob[0])
    for jj in range(1, STEPS):
        @pl.when(jj > j)
        def _(jj=jj):
            for kv in range(2):
                share(0, kv, jj).wait_recv()

        @pl.when(jj <= j)
        def _(jj=jj):
            ob[jj] = jnp.zeros_like(ob[jj])
    for copy in back:
        copy.wait()
    for p in range(HEADS):
        @pl.when(me != p)
        def _(p=p):
            for kv in range(2):
                deliver(p, kv, p).wait_recv()
    for kv in range(2):
        total = owns[kv][...] + xb[kv].astype(F32)
        for jj in range(1, STEPS):
            total = total + ob[jj, kv].astype(F32)
        outs[kv][...] = total.astype(BF16)
    for jj in range(STEPS):
        @pl.when(j == jj)
        def _(jj=jj):
            for p in range(HEADS):
                @pl.when(me != p)
                def _(p=p):
                    for kv in range(2):
                        collect(p, kv, me, jj).wait_send()
    for p in range(HEADS):
        @pl.when(me != p)
        def _(p=p):
            entropy(p, me).wait_send()
            for kv in range(2):
                deliver(p, kv, me).wait_send()
    for jj in range(STEPS - 1):
        @pl.when(jj < j)
        def _(jj=jj):
            for kv in range(2):
                share(jj, kv, j).wait_send()
    low.wait_send()
    high.wait_send()


def vmem(count):
    return [pl.BlockSpec(memory_space=pltpu.VMEM)] * count


def body(queries, keys, values, dout, doc_lengths, span_order):
    sem = pltpu.SemaphoreType.DMA
    smem = pl.BlockSpec(memory_space=pltpu.SMEM)
    width = HEADS * D
    pair = jax.ShapeDtypeStruct((2 * SPAN, width), BF16)
    kk, vv = pl.pallas_call(
        gather_kernel,
        out_shape=(pair, pair),
        in_specs=[smem] + vmem(2),
        out_specs=vmem(2),
        scratch_shapes=[
            pltpu.VMEM((2, 2 * SPAN, D), BF16),
            pltpu.VMEM((2, 2, SPAN, D), BF16),
            pltpu.VMEM((2, 2, SPAN, D), BF16),
            pltpu.VMEM((2, 2, SPAN, D), BF16),
            sem((HEADS, 2)), sem((HEADS, 2)), sem((STEPS, 2)), sem((STEPS, 2)),
            sem((2,)), sem((2,)), sem((HEADS, 2)), sem((HEADS, 2)), sem((4,)),
        ],
        compiler_params=pltpu.CompilerParams(collective_id=0, has_side_effects=True),
    )(span_order, keys, values)

    wide = pl.BlockSpec((ROWS, width), lambda h: (0, h))
    key_block = pl.BlockSpec((2 * SPAN, D), lambda h: (0, h))
    row_block = pl.BlockSpec((ROWS, D), lambda h: (0, h))
    tokens = jax.ShapeDtypeStruct((ROWS, HEADS * width), BF16)
    own_shape = jax.ShapeDtypeStruct((ROWS, width), F32)
    out, dq, gk, gv, ok, ov, ent = pl.pallas_call(
        attend_kernel,
        grid=(HEADS,),
        out_shape=(
            tokens, tokens, pair, pair, own_shape, own_shape,
            jax.ShapeDtypeStruct((HEADS, HEADS, D), F32),
        ),
        in_specs=[
            smem, pl.BlockSpec((1, D), lambda h: (0, 0)), wide, wide, key_block, key_block,
        ],
        out_specs=(
            wide, wide, key_block, key_block, row_block, row_block,
            pl.BlockSpec((1, HEADS, D), lambda h: (h, 0, 0)),
        ),
        scratch_shapes=[pltpu.VMEM((KEYS, D), F32)],
        compiler_params=pltpu.CompilerParams(dimension_semantics=("arbitrary",)),
    )(span_order, doc_lengths.reshape(1, D), queries, dout, kk, vv)

    grad = jax.ShapeDtypeStruct((ROWS, width), BF16)
    dk, dv, ent = pl.pallas_call(
        scatter_kernel,
        out_shape=(grad, grad, jax.ShapeDtypeStruct((HEADS, 2 * SPAN), F32)),
        in_specs=[smem] + vmem(5),
        out_specs=vmem(3),
        scratch_shapes=[
            pltpu.VMEM((HEADS, 2, SPAN, D), BF16),
            pltpu.VMEM((2, 2, SPAN, D), BF16),
            pltpu.VMEM((2, 2, SPAN, D), BF16),
            pltpu.VMEM((2, 2, SPAN, D), BF16),
            pltpu.VMEM((2, ROWS, width), BF16),
            pltpu.VMEM((STEPS, 2, ROWS, width), BF16),
            pltpu.VMEM((HEADS, HEADS, D), F32),
            sem((HEADS, 2)), sem((HEADS, 2)), sem((STEPS, 2)), sem((STEPS, 2)),
            sem((2,)), sem((2,)), sem((HEADS, 2)), sem((HEADS, 2)), sem((HEADS,)), sem((HEADS,)),
            sem((3,)),
        ],
        compiler_params=pltpu.CompilerParams(collective_id=1, has_side_effects=True),
    )(span_order, gk, gv, ok, ov, ent)
    return out, ent.T, dq, dk, dv


def solution(mesh):
    rows = P(("inner", "outer", "head"), None)
    return jax.shard_map(
        body,
        mesh=mesh,
        in_specs=(rows, rows, rows, rows, P(), P()),
        out_specs=(rows, P(("inner", "outer"), "head"), rows, rows, rows),
        check_vma=False,
    )
```

time: 254 us -> 86.2 us (0.34)
  the two profiles are of different devices: /device:TPU:100 before, /device:TPU:9 now
where the time goes in v1:
time: 86.2 us; the launch traced here: 85.9 us
  Pallas kernels  81.7 us (95%)
  local copies, waits for them, and re-layouts  3.59 us (4%)
    pallas_call x1, Pallas kernels, body(): pl.pallas_call(scatter_kernel, out_shape=(grad, grad, jax.ShapeDtypeStruc...  36.4 us
    pallas_call x1, Pallas kernels, body(): pl.pallas_call(gather_kernel, out_shape=(pair, pair), in_specs=[smem] + v...  32.7 us
    pallas_call x1, Pallas kernels, body(): pl.pallas_call(attend_kernel, grid=(HEADS,), out_shape=(tokens, tokens, p...  12.6 us
    unnamed x5, local copies, waits for them, and re-layouts  3.59 us

profile of v1, /device:TPU:9, one launch (start us, length us, event | category | flops | bytes accessed | tf_op | source)
XLA Modules:
  0.0 85.9 jit_solution(14408427433797883065)
XLA Ops:
  0.6 32.7 %shard_map.101 = (bf16[512,1024]{1,0:T(8,128)(2,1)}, bf16[512,1024]{1,0:T(8,128)(2,1)}) custom-call(s32[64]{0:T(128)} %order_ref.5, bf16[64,1024]{1,0:T(8,128)(2,1)} %k_ref.1, bf16[64,1024]{1,0:T(8,128)(2,1)} %v_ref.1), custom_call_target="tpu_custom_call" | custom-call | tf_op jit(solution)/shard_map/pallas_call | solution.py:411
  33.4 12.6 %shard_map.102 = (bf16[64,8192]{1,0:T(8,128)(2,1)}, bf16[64,8192]{1,0:T(8,128)(2,1)}, bf16[512,1024]{1,0:T(8,128)(2,1)}, bf16[512,1024]{1,0:T(8,128)(2,1)}, f32[...) custom-call(s32[64]{0:T(128)} %order_ref.5, s32[1,128]{1,0:T(1,128)} %bitcast.3, bf16[64,8192]{1,0:T(8,128)(2,1)} %q_ref.1, ...), custom_call_target="tpu_custom_call" | custom-call | tf_op jit(solution)/shard_map/pallas_call | solution.py:432
  46.0 36.4 %shard_map.103 = (bf16[64,1024]{1,0:T(8,128)(2,1)}, bf16[64,1024]{1,0:T(8,128)(2,1)}, f32[8,512]{1,0:T(8,128)}) custom-call(s32[64]{0:T(128)} %order_ref.5, bf16[512,1024]{1,0:T(8,128)(2,1)} %get-tuple-element.20.gk_ref, bf16[512,1024]{1,0:T(8,128)(2,1)} %get-tuple-element.21.gv_ref, f32[64,1024]{1,0:T(8,128)} %get-tuple-element.22.ok_ref, ...), custom_call_target="tpu_custom_call" | custom-call | tf_op jit(solution)/shard_map/pallas_call | solution.py:451
  82.3 1.3 %copy.14 = f32[512,8]{0,1:T(8,128)} copy(f32[512,8]{0,1:T(8,128)} %bitcast.2) | data formatting | bytes 32768
  83.7 0.0 copy-start
  83.7 1.6 %copy.15 = bf16[64,1024]{1,0:T(8,128)(2,1)} copy(bf16[64,1024]{1,0:T(8,128)(2,1)} %get-tuple-element.37) | data formatting | bytes 262144
  85.3 0.0 copy-done
  85.3 0.7 copy.16
Async XLA Ops:
  83.7 1.6 %copy-start = (bf16[64,1024]{1,0:T(8,128)(2,1)S(1)}, bf16[64,1024]{1,0:T(8,128)(2,1)}, u32[]{:S(2)}) copy-start(bf16[64,1024]{1,0:T(8,128)(2,1)} %get-tuple-element.38) | copy-start | bytes 393220

commit v2 on v0

v2 whole, which is shorter than its diff:
```python
import math

import jax
import jax.numpy as jnp
from jax import lax
from jax.experimental import pallas as pl
from jax.experimental.pallas import tpu as pltpu
from jax.sharding import PartitionSpec as P

MESH = pl.DeviceIdType.MESH
F32 = jnp.float32
BF16 = jnp.bfloat16
NEG = -1.0e30
LN2 = math.log(2.0)

D = 128
HEADS = 8
ROWS = 64
SPAN = 256
KEYS = 320
STEPS = SPAN // ROWS
PER = 4
SPLIT = 5
SPLIT_ROWS = 3
COPY_STEPS = 2


def place():
    me = lax.axis_index("head")
    outer_size = lax.axis_size("outer")
    cycle = lax.axis_size("inner") * outer_size
    own = lax.axis_index("inner") * outer_size + lax.axis_index("outer")

    def at(index):
        return {"inner": index // outer_size, "outer": lax.rem(index, outer_size)}

    above = at(lax.rem(own + 1, cycle))
    below = at(lax.rem(own + cycle - 1, cycle))
    return me, me // STEPS, lax.rem(me, STEPS), own, cycle, above, below


def greet(me, above, below):
    barrier = pltpu.get_barrier_semaphore()
    for step in range(1, HEADS):
        pl.semaphore_signal(
            barrier, inc=1, device_id={"head": lax.rem(me + step, HEADS)}, device_id_type=MESH
        )
    pl.semaphore_signal(barrier, inc=1, device_id=above, device_id_type=MESH)
    pl.semaphore_signal(barrier, inc=1, device_id=below, device_id_type=MESH)
    pl.semaphore_wait(barrier, HEADS + 1)


def remote(src, dst, send, recv, device):
    return pltpu.make_async_remote_copy(
        src_ref=src, dst_ref=dst, send_sem=send, recv_sem=recv, device_id=device, device_id_type=MESH
    )


def kernel(
    order_ref, len_ref, q_hbm, do_hbm, k_ref, v_ref,
    out_hbm, dq_hbm, dk_ref, dv_ref, ent_out,
    bias_ref, qs, dos, outs, dqs, kk, vv, gk, gv, own_grad, pf, pb, dsb,
    hb, nb, rb, sel, cb, tnb, trb, tsel, xb, ob, es, eb,
    s1_send, s1_recv, own_send, own_recv, s2_send, s2_recv, s3_send, s3_recv,
    t1_send, t1_recv, town_send, town_recv, t2_send, t2_recv, t3_send, t3_recv,
    e_send, e_recv, local, q_sem, o_sem,
):
    me, half, j, own, cycle, above, below = place()
    ins, keep, grads = (k_ref, v_ref), (kk, vv), (gk, gv)
    first_low = order_ref[2 * own] == own
    width = HEADS * D
    loads = []
    for h in range(HEADS):
        cols = pl.ds(h * width, width)
        loads.append(pltpu.make_async_copy(q_hbm.at[:, cols], qs.at[h], q_sem.at[0, h]))
        loads.append(pltpu.make_async_copy(do_hbm.at[:, cols], dos.at[h], q_sem.at[1, h]))
    for copy in loads:
        copy.start()

    def each(action):
        for p in range(HEADS):
            @pl.when(me != p)
            def _(p=p):
                action(p)

    def branch(action):
        for jj in range(STEPS):
            @pl.when(j == jj)
            def _(jj=jj):
                action(jj)

    def spread(p, kv, src):
        return remote(
            ins[kv].at[:, pl.ds(p * D, D)], hb.at[kv, pl.ds(src * ROWS, ROWS)],
            s1_send.at[p, kv], s1_recv.at[src, kv], {"head": p},
        )

    def share(jj, kv, src):
        return remote(
            ins[kv], keep[kv].at[pl.ds(SPAN + src * ROWS, ROWS)],
            own_send.at[jj, kv], own_recv.at[src, kv], {"head": half * STEPS + jj},
        )

    def pass_on(side, kv):
        return remote(
            nb.at[side, kv], rb.at[side, kv], s2_send.at[side, kv], s2_recv.at[side, kv],
            (above, below)[side],
        )

    def deliver(p, kv, src, jj):
        rows = pl.ds(jj * ROWS, SPAN - jj * ROWS)
        return remote(
            sel.at[p // STEPS, kv, rows], keep[kv].at[rows, pl.ds(src * D, D)],
            s3_send.at[p, kv], s3_recv.at[src, kv], {"head": p},
        )

    def collect(p, kv, src, jj):
        rows = pl.ds(jj * ROWS, SPAN - jj * ROWS)
        return remote(
            grads[kv].at[rows, pl.ds(p * D, D)], cb.at[src, kv, rows],
            t3_send.at[p, kv], t3_recv.at[src, kv], {"head": p},
        )

    def share_back(jj, kv, src):
        return remote(
            grads[kv].at[pl.ds(SPAN + jj * ROWS, ROWS)], ob.at[src, kv],
            town_send.at[jj, kv], town_recv.at[src, kv], {"head": half * STEPS + jj},
        )

    def pass_back(side, kv):
        return remote(
            tnb.at[side, kv], trb.at[side, kv], t2_send.at[side, kv], t2_recv.at[side, kv],
            (below, above)[side],
        )

    def give_back(p, kv, src):
        return remote(
            tsel.at[p // STEPS, kv, pl.ds((p % STEPS) * ROWS, ROWS)],
            xb.at[kv, :, pl.ds(src * D, D)],
            t1_send.at[p, kv], t1_recv.at[src, kv], {"head": p},
        )

    def entropy_to(p, src):
        return remote(es.at[p], eb.at[src], e_send.at[p], e_recv.at[src], {"head": p})

    greet(me, above, below)
    for kv in range(2):
        each(lambda p: spread(p, kv, me).start())
    mine = [
        pltpu.make_async_copy(
            ins[kv].at[:, pl.ds(me * D, D)], hb.at[kv, pl.ds(me * ROWS, ROWS)], local.at[kv]
        )
        for kv in range(2)
    ] + [
        pltpu.make_async_copy(
            ins[kv], keep[kv].at[pl.ds(SPAN + j * ROWS, ROWS)], local.at[2 + kv]
        )
        for kv in range(2)
    ]
    for copy in mine:
        copy.start()

    start_pos = order_ref[2 * own + half] * SPAN + j * ROWS
    lens = jnp.broadcast_to(len_ref[...], (D, D)).astype(F32)
    row = lax.broadcasted_iota(jnp.int32, (D, D), 0)
    col = lax.broadcasted_iota(jnp.int32, (D, D), 1)
    starts = jnp.sum(jnp.where(col < row, lens, 0.0), axis=1, keepdims=True)
    pos = (start_pos + lax.rem(col, ROWS)).astype(F32)
    found = jnp.max(jnp.where(starts <= pos, starts, 0.0), axis=0, keepdims=True)
    first = found - (start_pos - SPAN).astype(F32)
    key = lax.broadcasted_iota(jnp.int32, (KEYS, D), 0)
    query = lax.rem(lax.broadcasted_iota(jnp.int32, (KEYS, D), 1), ROWS)
    allowed = (key.astype(F32) >= first) & (key <= query + SPAN)
    bias_ref[...] = jnp.where(allowed, 0.0, NEG)
    for copy in mine:
        copy.wait()

    for kv in range(2):
        each(lambda p: spread(p, kv, p).wait_recv())
        a, b = hb[kv, :SPAN], hb[kv, SPAN:]
        nb[0, kv] = jnp.where(first_low, a, b)
        nb[1, kv] = jnp.where(first_low, b, a)
        pass_on(0, kv).start()
        pass_on(1, kv).start()
    for kv in range(2):
        for jj in range(1, STEPS):
            @pl.when(j < jj)
            def _(jj=jj):
                share(jj, kv, j).start()
    back = []
    for kv in range(2):
        pass_on(0, kv).wait_recv()
        pass_on(1, kv).wait_recv()
        prev_low = rb[0, kv]
        prev_high = jnp.where(own == cycle - 1, nb[0, kv], rb[1, kv])
        sel[0, kv] = jnp.where(first_low, prev_low, prev_high)
        sel[1, kv] = jnp.where(first_low, prev_high, prev_low)
        each(lambda p: deliver(p, kv, me, p % STEPS).start())
        copy = pltpu.make_async_copy(
            sel.at[half, kv], keep[kv].at[pl.ds(0, SPAN), pl.ds(me * D, D)], local.at[kv]
        )
        copy.start()
        back.append(copy)

    def wait_own(kv):
        for jj in range(STEPS - 1):
            @pl.when(jj < j)
            def _(jj=jj):
                share(0, kv, jj).wait_recv()

    scale = 1.0 / math.sqrt(D)
    nt = (((1,), (1,)), ((), ()))
    nn = (((1,), (0,)), ((), ()))
    lanes = PER * ROWS
    rows = pl.multiple_of(j * ROWS, ROWS)
    window = pl.ds(rows, KEYS)
    sub = lax.broadcasted_iota(jnp.int32, (HEADS, D), 0)

    def columns(h):
        return pl.ds(pl.multiple_of(h * D, D), D)

    def stacked(ref, h, chunk):
        return jnp.concatenate(
            [ref[h, :, g * D : (g + 1) * D] for g in range(chunk * PER, (chunk + 1) * PER)], axis=0
        )

    def arrive(step, h, kv):
        @pl.when(step > 0)
        def _():
            branch(lambda jj: deliver(h, kv, h, jj).wait_recv())

    def leave(step, h, kv):
        @pl.when(step > 0)
        def _():
            branch(lambda jj: collect(h, kv, me, jj).start())

    def store_grad(kv, h, total):
        grads[kv][pl.ds(rows, SPAN), columns(h)] = total[:SPAN].astype(BF16)
        own_grad[kv, :, columns(h)] = total[SPAN:]

    def score_step(step, carry):
        h = lax.rem(me + step, HEADS)
        arrive(step, h, 0)
        k5 = kk[window, columns(h)]
        bias = jnp.concatenate([bias_ref[...]] * (lanes // D), axis=1)
        ent = jnp.zeros((HEADS, D), F32)
        dv = jnp.zeros((KEYS, D), F32)
        for chunk in range(HEADS // PER):
            at = slice(chunk * lanes, (chunk + 1) * lanes)
            q, do = stacked(qs, h, chunk), stacked(dos, h, chunk)
            t = lax.dot_general(k5, q, nt, preferred_element_type=F32) * (scale / LN2) + bias
            u = t - jnp.max(t, axis=0, keepdims=True)
            e = jnp.exp2(u)
            total = jnp.sum(e, axis=0, keepdims=True)
            p = e * (1.0 / total)
            spread_sum = jnp.sum(p * u, axis=0, keepdims=True)
            entropy = LN2 * (jnp.log2(total) - spread_sum)
            pf[h, :, at] = p
            rounded = p.astype(BF16)
            pb[h, :, at] = rounded
            dv = dv + lax.dot_general(rounded, do, nn, preferred_element_type=F32)
            for n in range(PER // 2):
                pair = jnp.broadcast_to(entropy[:, n * D : (n + 1) * D], (HEADS, D))
                g = chunk * PER + 2 * n
                ent = jnp.where(sub == g, pair, ent)
                ent = jnp.where(sub == g + 1, pltpu.roll(pair, ROWS, 1), ent)
        es[h] = ent
        store_grad(1, h, dv)
        leave(step, h, 1)

        @pl.when(step > 0)
        def _():
            entropy_to(h, me).start()

        return carry

    def slope_step(step, carry):
        h = lax.rem(me + step, HEADS)
        arrive(step, h, 1)
        v5 = vv[window, columns(h)]
        dk = jnp.zeros((KEYS, D), F32)
        for chunk in range(HEADS // PER):
            at = slice(chunk * lanes, (chunk + 1) * lanes)
            q, do = stacked(qs, h, chunk), stacked(dos, h, chunk)
            dp = lax.dot_general(v5, do, nt, preferred_element_type=F32)
            p = pf[h, :, at]
            delta = jnp.sum(p * dp, axis=0, keepdims=True)
            ds = (p * ((dp - delta) * scale)).astype(BF16)
            dsb[h, :, at] = ds
            dk = dk + lax.dot_general(ds, q, nn, preferred_element_type=F32)
        store_grad(0, h, dk)
        leave(step, h, 0)
        return carry

    def stores(h):
        cols = pl.ds(pl.multiple_of(h * width, width), width)
        return (
            pltpu.make_async_copy(outs.at[h], out_hbm.at[:, cols], o_sem.at[0, h]),
            pltpu.make_async_copy(dqs.at[h], dq_hbm.at[:, cols], o_sem.at[1, h]),
        )

    def row_step(h, carry):
        k5t, v5t = kk[window, columns(h)].T, vv[window, columns(h)].T
        for chunk in range(HEADS // PER):
            at = slice(chunk * lanes, (chunk + 1) * lanes)
            out = lax.dot_general(v5t, pb[h, :, at], nn, preferred_element_type=F32).T
            dq = lax.dot_general(k5t, dsb[h, :, at], nn, preferred_element_type=F32).T
            for n in range(PER):
                g = chunk * PER + n
                outs[h, :, g * D : (g + 1) * D] = out[n * ROWS : (n + 1) * ROWS].astype(BF16)
                dqs[h, :, g * D : (g + 1) * D] = dq[n * ROWS : (n + 1) * ROWS].astype(BF16)
        for copy in stores(h):
            copy.start()
        return carry

    def summed(kv):
        sides = []
        for side in range(2):
            blocks = []
            for b in range(STEPS):
                at = slice(b * ROWS, (b + 1) * ROWS)
                total = cb[side * STEPS, kv, at].astype(F32)
                for jj in range(1, b + 1):
                    total = total + cb[side * STEPS + jj, kv, at].astype(F32)
                blocks.append(total.astype(BF16))
            sides.append(jnp.concatenate(blocks, axis=0))
        tnb[0, kv] = jnp.where(first_low, sides[0], sides[1])
        tnb[1, kv] = jnp.where(first_low, sides[1], sides[0])

    def keep_mine(kv):
        return pltpu.make_async_copy(
            grads[kv].at[pl.ds(0, SPAN), pl.ds(me * D, D)], cb.at[me, kv], local.at[5 + kv]
        )

    def send_sums(kv):
        each(lambda p: collect(p, kv, p, p % STEPS).wait_recv())
        keep_mine(kv).wait()
        summed(kv)
        pass_back(0, kv).start()
        pass_back(1, kv).start()

    def send_shares(kv):
        for jj in range(STEPS - 1):
            @pl.when(jj < j)
            def _(jj=jj):
                share_back(jj, kv, j).start()

    def keep_given(kv):
        return pltpu.make_async_copy(
            tsel.at[half, kv, pl.ds(j * ROWS, ROWS)], xb.at[kv, :, pl.ds(me * D, D)],
            local.at[2 + kv],
        )

    def send_given(kv):
        pass_back(0, kv).wait_recv()
        pass_back(1, kv).wait_recv()
        low_part = jnp.where(own == cycle - 1, tnb[1, kv], trb[0, kv])
        high_part = jnp.where(own == 0, jnp.zeros_like(trb[1, kv]), trb[1, kv])
        tsel[0, kv] = jnp.where(first_low, low_part, high_part)
        tsel[1, kv] = jnp.where(first_low, high_part, low_part)
        each(lambda p: give_back(p, kv, me).start())
        keep_given(kv).start()

    def finish(kv, dst):
        ob[0, kv] = jnp.zeros_like(ob[0, kv])
        for jj in range(1, STEPS):
            @pl.when(jj > j)
            def _(jj=jj):
                share_back(0, kv, jj).wait_recv()

            @pl.when(jj <= j)
            def _(jj=jj):
                ob[jj, kv] = jnp.zeros_like(ob[jj, kv])
        keep_given(kv).wait()
        each(lambda p: give_back(p, kv, p).wait_recv())
        total = own_grad[kv] + xb[kv].astype(F32)
        for jj in range(1, STEPS):
            total = total + ob[jj, kv].astype(F32)
        dst[...] = total.astype(BF16)

    for copy in loads:
        copy.wait()
    wait_own(0)
    back[0].wait()
    lax.fori_loop(0, HEADS, score_step, 0)
    keep_mine(1).start()
    send_shares(1)
    wait_own(1)
    back[1].wait()
    lax.fori_loop(0, SPLIT, slope_step, 0)
    send_sums(1)
    lax.fori_loop(SPLIT, HEADS, slope_step, 0)
    keep_mine(0).start()
    send_shares(0)
    lax.fori_loop(0, SPLIT_ROWS, row_step, 0)
    send_sums(0)
    send_given(1)
    lax.fori_loop(SPLIT_ROWS, HEADS, row_step, 0)
    send_given(0)
    finish(1, dv_ref)
    local_ent = pltpu.make_async_copy(es.at[me], eb.at[me], local.at[4])
    local_ent.start()
    local_ent.wait()
    each(lambda p: entropy_to(p, p).wait_recv())
    for n in range(HEADS // 2):
        ent_out[:, n * D : n * D + ROWS] = eb[2 * n, :, :ROWS]
        ent_out[:, n * D + ROWS : (n + 1) * D] = eb[2 * n + 1, :, :ROWS]
    finish(0, dk_ref)
    for kv in range(2):
        branch(lambda jj: each(lambda p: collect(p, kv, me, jj).wait_send()))

        def sent(p):
            spread(p, kv, me).wait_send()
            deliver(p, kv, me, p % STEPS).wait_send()
            give_back(p, kv, me).wait_send()

        each(sent)
        for jj in range(STEPS):
            if jj > 0:
                @pl.when(j < jj)
                def _(jj=jj):
                    share(jj, kv, j).wait_send()

            if jj < STEPS - 1:
                @pl.when(jj < j)
                def _(jj=jj):
                    share_back(jj, kv, j).wait_send()

        for side in range(2):
            pass_on(side, kv).wait_send()
            pass_back(side, kv).wait_send()
    each(lambda p: entropy_to(p, me).wait_send())
    for h in range(HEADS):
        for copy in stores(h):
            copy.wait()


def copy_kernel(*refs):
    count = len(refs) // 2
    for src, dst in zip(refs[:count], refs[count:]):
        dst[...] = src[...]


def body(queries, keys, values, dout, doc_lengths, span_order):
    sem = pltpu.SemaphoreType.DMA
    smem = pl.BlockSpec(memory_space=pltpu.SMEM)
    hbm = pl.BlockSpec(memory_space=pl.ANY)
    whole = pl.BlockSpec(memory_space=pltpu.VMEM)
    width = HEADS * D
    lanes = HEADS * ROWS
    tokens = jax.ShapeDtypeStruct((ROWS, HEADS * width), BF16)
    grad = jax.ShapeDtypeStruct((ROWS, width), BF16)
    entropy = jax.ShapeDtypeStruct((HEADS, 2 * SPAN), F32)
    side = pltpu.VMEM((2, 2, SPAN, D), BF16)
    results = pl.pallas_call(
        kernel,
        out_shape=(tokens, tokens, grad, grad, entropy),
        in_specs=[smem, whole, hbm, hbm, whole, whole],
        out_specs=(hbm, hbm, whole, whole, whole),
        scratch_shapes=[
            pltpu.VMEM((KEYS, D), F32),
            pltpu.VMEM((HEADS, ROWS, width), BF16),
            pltpu.VMEM((HEADS, ROWS, width), BF16),
            pltpu.VMEM((HEADS, ROWS, width), BF16),
            pltpu.VMEM((HEADS, ROWS, width), BF16),
            pltpu.VMEM((2 * SPAN, width), BF16),
            pltpu.VMEM((2 * SPAN, width), BF16),
            pltpu.VMEM((2 * SPAN, width), BF16),
            pltpu.VMEM((2 * SPAN, width), BF16),
            pltpu.VMEM((2, ROWS, width), F32),
            pltpu.VMEM((HEADS, KEYS, lanes), F32),
            pltpu.VMEM((HEADS, KEYS, lanes), BF16),
            pltpu.VMEM((HEADS, KEYS, lanes), BF16),
            pltpu.VMEM((2, 2 * SPAN, D), BF16),
            side, side, side,
            pltpu.VMEM((HEADS, 2, SPAN, D), BF16),
            side, side, side,
            pltpu.VMEM((2, ROWS, width), BF16),
            pltpu.VMEM((STEPS, 2, ROWS, width), BF16),
            pltpu.VMEM((HEADS, HEADS, D), F32),
            pltpu.VMEM((HEADS, HEADS, D), F32),
            sem((HEADS, 2)), sem((HEADS, 2)), sem((STEPS, 2)), sem((STEPS, 2)),
            sem((2, 2)), sem((2, 2)), sem((HEADS, 2)), sem((HEADS, 2)),
            sem((HEADS, 2)), sem((HEADS, 2)), sem((STEPS, 2)), sem((STEPS, 2)),
            sem((2, 2)), sem((2, 2)), sem((HEADS, 2)), sem((HEADS, 2)),
            sem((HEADS,)), sem((HEADS,)), sem((7,)), sem((2, HEADS)), sem((2, HEADS)),
        ],
        compiler_params=pltpu.CompilerParams(collective_id=0, has_side_effects=True),
    )(span_order, doc_lengths.reshape(1, D), queries, dout, keys, values)
    if COPY_STEPS:
        blocks = [
            pl.BlockSpec((s.shape[0], s.shape[1] // COPY_STEPS), lambda n: (0, n))
            for s in (tokens, tokens, grad, grad, entropy)
        ]
        results = pl.pallas_call(
            copy_kernel,
            grid=(COPY_STEPS,),
            out_shape=(tokens, tokens, grad, grad, entropy),
            in_specs=blocks,
            out_specs=tuple(blocks),
        )(*results)
    out, dq, dk, dv, ent = results
    return out, ent.T, dq, dk, dv


def solution(mesh):
    rows = P(("inner", "outer", "head"), None)
    return jax.shard_map(
        body,
        mesh=mesh,
        in_specs=(rows, rows, rows, rows, P(), P()),
        out_specs=(rows, P(("inner", "outer"), "head"), rows, rows, rows),
        check_vma=False,
    )
```

time: 254 us -> 63.3 us (0.25)
  the two profiles are of different devices: /device:TPU:100 before, /device:TPU:1 now
where the time goes in v2:
time: 63.3 us; the launch traced here: 63.2 us
  Pallas kernels  62.5 us (99%)
  between operations  0.64 us (1%)
    pallas_call x1, Pallas kernels, body(): pl.pallas_call(kernel, out_shape=(tokens, tokens, grad, grad, entropy), i...  59.8 us
    pallas_call x1, Pallas kernels, body(): pl.pallas_call(copy_kernel, grid=(COPY_STEPS,), out_shape=(tokens, tokens...  2.72 us

profile of v2, /device:TPU:1, one launch (start us, length us, event | category | flops | bytes accessed | tf_op | source)
XLA Modules:
  0.0 63.2 jit_solution(10110822833208454388)
XLA Ops:
  0.6 59.8 %shard_map.101 = (bf16[64,8192]{1,0:T(8,128)(2,1)}, bf16[64,8192]{1,0:T(8,128)(2,1)}, bf16[64,1024]{1,0:T(8,128)(2,1)}, bf16[64,1024]{1,0:T(8,128)(2,1)}, f32[8,512]{1,0:T(8,128)}) custom-call(s32[64]{0:T(128)} %order_ref.1, s32[1,128]{1,0:T(1,128)} %bitcast.2, bf16[64,8192]{1,0:T(8,128)(2,1)} %q_hbm.1, bf16[64,8192]{1,0:T(8,128)(2,1)} %do_hbm.1, ...), custom_call_target="tpu_custom_call" | custom-call | tf_op jit(solution)/shard_map/pallas_call | solution.py:455
  60.5 2.7 %shard_map.102 = (bf16[64,8192]{1,0:T(8,128)(2,1)}, bf16[64,8192]{1,0:T(8,128)(2,1)}, bf16[64,1024]{1,0:T(8,128)(2,1)}, bf16[64,1024]{1,0:T(8,128)(2,1)}, f32[8,512]{1,0:T(8,128)}) custom-call(bf16[64,8192]{1,0:T(8,128)(2,1)} %get-tuple-element.15.refs_0_, bf16[64,8192]{1,0:T(8,128)(2,1)} %get-tuple-element.16.refs_1_, ...), custom_call_target="tpu_custom_call" | custom-call | tf_op jit(solution)/shard_map/pallas_call | solution.py:495

commit v3 on v2

--- a/solution.py
+++ b/solution.py
@@ -20,9 +20,9 @@
 KEYS = 320
 STEPS = SPAN // ROWS
 PER = 4
-SPLIT = 5
+SPLIT = 6
 SPLIT_ROWS = 3
-COPY_STEPS = 2
+VMEM_LIMIT = 40 << 20
 
 
 def place():
@@ -57,19 +57,24 @@
 
 
 def kernel(
-    order_ref, len_ref, q_hbm, do_hbm, k_ref, v_ref,
-    out_hbm, dq_hbm, dk_ref, dv_ref, ent_out,
-    bias_ref, qs, dos, outs, dqs, kk, vv, gk, gv, own_grad, pf, pb, dsb,
+    order_hbm, len_hbm, q_hbm, do_hbm, k_ref, v_ref,
+    outs, dqs, dk_ref, dv_ref, ent_out,
+    order_ref, len_ref, bias_ref, qs, dos, kk, vv, gk, gv, own_grad, pf, pb, dsb,
     hb, nb, rb, sel, cb, tnb, trb, tsel, xb, ob, es, eb,
     s1_send, s1_recv, own_send, own_recv, s2_send, s2_recv, s3_send, s3_recv,
     t1_send, t1_recv, town_send, town_recv, t2_send, t2_recv, t3_send, t3_recv,
-    e_send, e_recv, local, q_sem, o_sem,
+    e_send, e_recv, local, q_sem,
 ):
     me, half, j, own, cycle, above, below = place()
     ins, keep, grads = (k_ref, v_ref), (kk, vv), (gk, gv)
-    first_low = order_ref[2 * own] == own
     width = HEADS * D
     loads = []
+    facts = [
+        pltpu.make_async_copy(order_hbm, order_ref, local.at[11]),
+        pltpu.make_async_copy(len_hbm, len_ref, local.at[12]),
+    ]
+    for copy in facts:
+        copy.start()
     for h in range(HEADS):
         cols = pl.ds(h * width, width)
         loads.append(pltpu.make_async_copy(q_hbm.at[:, cols], qs.at[h], q_sem.at[0, h]))
@@ -89,16 +94,29 @@
             def _(jj=jj):
                 action(jj)
 
+    def later(action):
+        for jj in range(1, STEPS):
+            @pl.when(j == jj)
+            def _(jj=jj):
+                action(jj)
+
     def spread(p, kv, src):
         return remote(
             ins[kv].at[:, pl.ds(p * D, D)], hb.at[kv, pl.ds(src * ROWS, ROWS)],
             s1_send.at[p, kv], s1_recv.at[src, kv], {"head": p},
         )
 
-    def share(jj, kv, src):
-        return remote(
-            ins[kv], keep[kv].at[pl.ds(SPAN + src * ROWS, ROWS)],
-            own_send.at[jj, kv], own_recv.at[src, kv], {"head": half * STEPS + jj},
+    def share(p, kv, src, jj):
+        return remote(
+            hb.at[kv, pl.ds((p // STEPS) * SPAN, jj * ROWS)],
+            keep[kv].at[pl.ds(SPAN, jj * ROWS), pl.ds(src * D, D)],
+            own_send.at[p, kv], own_recv.at[src, kv], {"head": p},
+        )
+
+    def share_mine(kv, jj):
+        return pltpu.make_async_copy(
+            hb.at[kv, pl.ds(half * SPAN, jj * ROWS)],
+            keep[kv].at[pl.ds(SPAN, jj * ROWS), pl.ds(me * D, D)], local.at[7 + kv],
         )
 
     def pass_on(side, kv):
@@ -121,10 +139,17 @@
             t3_send.at[p, kv], t3_recv.at[src, kv], {"head": p},
         )
 
-    def share_back(jj, kv, src):
-        return remote(
-            grads[kv].at[pl.ds(SPAN + jj * ROWS, ROWS)], ob.at[src, kv],
-            town_send.at[jj, kv], town_recv.at[src, kv], {"head": half * STEPS + jj},
+    def share_back(p, kv, src, jj):
+        return remote(
+            grads[kv].at[pl.ds(SPAN, jj * ROWS), pl.ds(p * D, D)],
+            ob.at[src, kv, pl.ds(0, jj * ROWS)],
+            town_send.at[p, kv], town_recv.at[src, kv], {"head": p},
+        )
+
+    def share_back_mine(kv, jj):
+        return pltpu.make_async_copy(
+            grads[kv].at[pl.ds(SPAN, jj * ROWS), pl.ds(me * D, D)],
+            ob.at[me, kv, pl.ds(0, jj * ROWS)], local.at[9 + kv],
         )
 
     def pass_back(side, kv):
@@ -160,6 +185,9 @@
     for copy in mine:
         copy.start()
 
+    for copy in facts:
+        copy.wait()
+    first_low = order_ref[2 * own] == own
     start_pos = order_ref[2 * own + half] * SPAN + j * ROWS
     lens = jnp.broadcast_to(len_ref[...], (D, D)).astype(F32)
     row = lax.broadcasted_iota(jnp.int32, (D, D), 0)
@@ -183,10 +211,8 @@
         pass_on(0, kv).start()
         pass_on(1, kv).start()
     for kv in range(2):
-        for jj in range(1, STEPS):
-            @pl.when(j < jj)
-            def _(jj=jj):
-                share(jj, kv, j).start()
+        later(lambda jj: share_mine(kv, jj).start())
+        each(lambda p: share(p, kv, me, p % STEPS).start() if p % STEPS else None)
     back = []
     for kv in range(2):
         pass_on(0, kv).wait_recv()
@@ -202,12 +228,6 @@
         copy.start()
         back.append(copy)
 
-    def wait_own(kv):
-        for jj in range(STEPS - 1):
-            @pl.when(jj < j)
-            def _(jj=jj):
-                share(0, kv, jj).wait_recv()
-
     scale = 1.0 / math.sqrt(D)
     nt = (((1,), (1,)), ((), ()))
     nn = (((1,), (0,)), ((), ()))
@@ -228,6 +248,7 @@
         @pl.when(step > 0)
         def _():
             branch(lambda jj: deliver(h, kv, h, jj).wait_recv())
+            later(lambda jj: share(h, kv, h, jj).wait_recv())
 
     def leave(step, h, kv):
         @pl.when(step > 0)
@@ -292,13 +313,6 @@
         leave(step, h, 0)
         return carry
 
-    def stores(h):
-        cols = pl.ds(pl.multiple_of(h * width, width), width)
-        return (
-            pltpu.make_async_copy(outs.at[h], out_hbm.at[:, cols], o_sem.at[0, h]),
-            pltpu.make_async_copy(dqs.at[h], dq_hbm.at[:, cols], o_sem.at[1, h]),
-        )
-
     def row_step(h, carry):
         k5t, v5t = kk[window, columns(h)].T, vv[window, columns(h)].T
         for chunk in range(HEADS // PER):
@@ -309,8 +323,6 @@
                 g = chunk * PER + n
                 outs[h, :, g * D : (g + 1) * D] = out[n * ROWS : (n + 1) * ROWS].astype(BF16)
                 dqs[h, :, g * D : (g + 1) * D] = dq[n * ROWS : (n + 1) * ROWS].astype(BF16)
-        for copy in stores(h):
-            copy.start()
         return carry
 
     def summed(kv):
@@ -340,10 +352,18 @@
         pass_back(1, kv).start()
 
     def send_shares(kv):
-        for jj in range(STEPS - 1):
-            @pl.when(jj < j)
-            def _(jj=jj):
-                share_back(jj, kv, j).start()
+        later(lambda jj: share_back_mine(kv, jj).start())
+        later(lambda jj: each(lambda p: share_back(p, kv, me, jj).start()))
+
+    def own_sum(kv, side):
+        blocks = []
+        for b in range(STEPS):
+            at = slice(b * ROWS, (b + 1) * ROWS)
+            total = jnp.zeros((ROWS, D), F32)
+            for jj in range(b + 1, STEPS):
+                total = total + ob[side * STEPS + jj, kv, at].astype(F32)
+            blocks.append(total)
+        return jnp.concatenate(blocks, axis=0)
 
     def keep_given(kv):
         return pltpu.make_async_copy(
@@ -352,41 +372,33 @@
         )
 
     def send_given(kv):
+        each(lambda p: share_back(p, kv, p, p % STEPS).wait_recv() if p % STEPS else None)
+        later(lambda jj: share_back_mine(kv, jj).wait())
         pass_back(0, kv).wait_recv()
         pass_back(1, kv).wait_recv()
-        low_part = jnp.where(own == cycle - 1, tnb[1, kv], trb[0, kv])
-        high_part = jnp.where(own == 0, jnp.zeros_like(trb[1, kv]), trb[1, kv])
-        tsel[0, kv] = jnp.where(first_low, low_part, high_part)
-        tsel[1, kv] = jnp.where(first_low, high_part, low_part)
+        low_part = jnp.where(own == cycle - 1, tnb[1, kv], trb[0, kv]).astype(F32)
+        high_part = jnp.where(own == 0, jnp.zeros_like(trb[1, kv]), trb[1, kv]).astype(F32)
+        first_part = jnp.where(first_low, low_part, high_part) + own_sum(kv, 0)
+        second_part = jnp.where(first_low, high_part, low_part) + own_sum(kv, 1)
+        tsel[0, kv] = first_part.astype(BF16)
+        tsel[1, kv] = second_part.astype(BF16)
         each(lambda p: give_back(p, kv, me).start())
         keep_given(kv).start()
 
     def finish(kv, dst):
-        ob[0, kv] = jnp.zeros_like(ob[0, kv])
-        for jj in range(1, STEPS):
-            @pl.when(jj > j)
-            def _(jj=jj):
-                share_back(0, kv, jj).wait_recv()
-
-            @pl.when(jj <= j)
-            def _(jj=jj):
-                ob[jj, kv] = jnp.zeros_like(ob[jj, kv])
         keep_given(kv).wait()
         each(lambda p: give_back(p, kv, p).wait_recv())
-        total = own_grad[kv] + xb[kv].astype(F32)
-        for jj in range(1, STEPS):
-            total = total + ob[jj, kv].astype(F32)
-        dst[...] = total.astype(BF16)
+        dst[...] = (own_grad[kv] + xb[kv].astype(F32)).astype(BF16)
 
     for copy in loads:
         copy.wait()
-    wait_own(0)
     back[0].wait()
+    later(lambda jj: share_mine(0, jj).wait())
     lax.fori_loop(0, HEADS, score_step, 0)
     keep_mine(1).start()
     send_shares(1)
-    wait_own(1)
     back[1].wait()
+    later(lambda jj: share_mine(1, jj).wait())
     lax.fori_loop(0, SPLIT, slope_step, 0)
     send_sums(1)
     lax.fori_loop(SPLIT, HEADS, slope_step, 0)
@@ -413,54 +425,53 @@
             spread(p, kv, me).wait_send()
             deliver(p, kv, me, p % STEPS).wait_send()
             give_back(p, kv, me).wait_send()
+            if p % STEPS:
+                share(p, kv, me, p % STEPS).wait_send()
 
         each(sent)
-        for jj in range(STEPS):
-            if jj > 0:
-                @pl.when(j < jj)
-                def _(jj=jj):
-                    share(jj, kv, j).wait_send()
-
-            if jj < STEPS - 1:
-                @pl.when(jj < j)
-                def _(jj=jj):
-                    share_back(jj, kv, j).wait_send()
-
+        later(lambda jj: each(lambda p: share_back(p, kv, me, jj).wait_send()))
         for side in range(2):
             pass_on(side, kv).wait_send()
             pass_back(side, kv).wait_send()
     each(lambda p: entropy_to(p, me).wait_send())
+
+
+def write_kernel(outs, dqs, dk, dv, ent, out_hbm, dq_hbm, dk_hbm, dv_hbm, ent_hbm, sems):
+    width = HEADS * D
+    copies = [
+        pltpu.make_async_copy(src, dst, sems.at[n])
+        for n, (src, dst) in enumerate(((dk, dk_hbm), (dv, dv_hbm), (ent, ent_hbm)))
+    ]
     for h in range(HEADS):
-        for copy in stores(h):
-            copy.wait()
-
-
-def copy_kernel(*refs):
-    count = len(refs) // 2
-    for src, dst in zip(refs[:count], refs[count:]):
-        dst[...] = src[...]
+        cols = pl.ds(h * width, width)
+        copies.append(pltpu.make_async_copy(outs.at[h], out_hbm.at[:, cols], sems.at[3 + 2 * h]))
+        copies.append(pltpu.make_async_copy(dqs.at[h], dq_hbm.at[:, cols], sems.at[4 + 2 * h]))
+    for copy in copies:
+        copy.start()
+    for copy in copies:
+        copy.wait()
 
 
 def body(queries, keys, values, dout, doc_lengths, span_order):
     sem = pltpu.SemaphoreType.DMA
-    smem = pl.BlockSpec(memory_space=pltpu.SMEM)
     hbm = pl.BlockSpec(memory_space=pl.ANY)
     whole = pl.BlockSpec(memory_space=pltpu.VMEM)
     width = HEADS * D
     lanes = HEADS * ROWS
+    stacked = jax.ShapeDtypeStruct((HEADS, ROWS, width), BF16)
     tokens = jax.ShapeDtypeStruct((ROWS, HEADS * width), BF16)
     grad = jax.ShapeDtypeStruct((ROWS, width), BF16)
     entropy = jax.ShapeDtypeStruct((HEADS, 2 * SPAN), F32)
     side = pltpu.VMEM((2, 2, SPAN, D), BF16)
     results = pl.pallas_call(
         kernel,
-        out_shape=(tokens, tokens, grad, grad, entropy),
-        in_specs=[smem, whole, hbm, hbm, whole, whole],
-        out_specs=(hbm, hbm, whole, whole, whole),
+        out_shape=(stacked, stacked, grad, grad, entropy),
+        in_specs=[pl.BlockSpec(memory_space=pltpu.HBM)] * 6,
+        out_specs=(whole, whole, whole, whole, whole),
         scratch_shapes=[
+            pltpu.SMEM((span_order.shape[0],), jnp.int32),
+            pltpu.VMEM((1, D), jnp.int32),
             pltpu.VMEM((KEYS, D), F32),
-            pltpu.VMEM((HEADS, ROWS, width), BF16),
-            pltpu.VMEM((HEADS, ROWS, width), BF16),
             pltpu.VMEM((HEADS, ROWS, width), BF16),
             pltpu.VMEM((HEADS, ROWS, width), BF16),
             pltpu.VMEM((2 * SPAN, width), BF16),
@@ -476,29 +487,30 @@
             pltpu.VMEM((HEADS, 2, SPAN, D), BF16),
             side, side, side,
             pltpu.VMEM((2, ROWS, width), BF16),
-            pltpu.VMEM((STEPS, 2, ROWS, width), BF16),
+            pltpu.VMEM((HEADS, 2, SPAN, D), BF16),
             pltpu.VMEM((HEADS, HEADS, D), F32),
             pltpu.VMEM((HEADS, HEADS, D), F32),
-            sem((HEADS, 2)), sem((HEADS, 2)), sem((STEPS, 2)), sem((STEPS, 2)),
+            sem((HEADS, 2)), sem((HEADS, 2)), sem((HEADS, 2)), sem((HEADS, 2)),
             sem((2, 2)), sem((2, 2)), sem((HEADS, 2)), sem((HEADS, 2)),
-            sem((HEADS, 2)), sem((HEADS, 2)), sem((STEPS, 2)), sem((STEPS, 2)),
+            sem((HEADS, 2)), sem((HEADS, 2)), sem((HEADS, 2)), sem((HEADS, 2)),
             sem((2, 2)), sem((2, 2)), sem((HEADS, 2)), sem((HEADS, 2)),
-            sem((HEADS,)), sem((HEADS,)), sem((7,)), sem((2, HEADS)), sem((2, HEADS)),
+            sem((HEADS,)), sem((HEADS,)), sem((13,)), sem((2, HEADS)),
         ],
-        compiler_params=pltpu.CompilerParams(collective_id=0, has_side_effects=True),
-    )(span_order, doc_lengths.reshape(1, D), queries, dout, keys, values)
-    if COPY_STEPS:
-        blocks = [
-            pl.BlockSpec((s.shape[0], s.shape[1] // COPY_STEPS), lambda n: (0, n))
-            for s in (tokens, tokens, grad, grad, entropy)
+        compiler_params=pltpu.CompilerParams(collective_id=0, has_side_effects=True, vmem_limit_bytes=VMEM_LIMIT),
+    )(
+        *[
+            pltpu.with_memory_space_constraint(x, pltpu.HBM)
+            for x in (span_order, doc_lengths.reshape(1, D), queries, dout, keys, values)
         ]
-        results = pl.pallas_call(
-            copy_kernel,
-            grid=(COPY_STEPS,),
-            out_shape=(tokens, tokens, grad, grad, entropy),
-            in_specs=blocks,
-            out_specs=tuple(blocks),
-        )(*results)
+    )
+    results = pl.pallas_call(
+        write_kernel,
+        out_shape=(tokens, tokens, grad, grad, entropy),
+        in_specs=[whole] * 5,
+        out_specs=(hbm, hbm, hbm, hbm, hbm),
+        scratch_shapes=[sem((3 + 2 * HEADS,))],
+        compiler_params=pltpu.CompilerParams(vmem_limit_bytes=8 << 20),
+    )(*results)
     out, dq, dk, dv, ent = results
     return out, ent.T, dq, dk, dv
 

time: 63.3 us -> 56 us (0.88)
  Pallas kernels: 62.5 us -> 55.2 us
    pallas_call x2, Pallas kernels: 62.5 us -> 55.2 us  [the longest x1 53.6 us: body(): pl.pallas_call(kernel, out_shape=(stacked, stacked, grad, grad, entropy),...]
where the time goes in v3:
time: 56 us; the launch traced here: 55.8 us
  Pallas kernels  55.2 us (99%)
  between operations  0.64 us (1%)
    pallas_call x1, Pallas kernels, body(): pl.pallas_call(kernel, out_shape=(stacked, stacked, grad, grad, entropy),...  53.6 us
    pallas_call x1, Pallas kernels, body(): pl.pallas_call(write_kernel, out_shape=(tokens, tokens, grad, grad, entro...  1.56 us

profile of v3, /device:TPU:1, one launch (start us, length us, event | category | flops | bytes accessed | tf_op | source)
XLA Modules:
  0.0 55.8 jit_solution(2204571521816611348)
XLA Ops:
  0.6 53.6 %shard_map.101 = (bf16[8,64,1024]{2,1,0:T(8,128)(2,1)S(1)}, bf16[8,64,1024]{2,1,0:T(8,128)(2,1)S(1)}, bf16[64,1024]{1,0:T(8,128)(2,1)S(1)}, bf16[64,1024]{1,0:T(8,128)(2,1)S(1)}, f32[8,512]{1,0:T(8,128)S(1)}) custom-call(s32[64]{0:T(128)} %order_hbm.1, s32[1,128]{1,0:T(1,128)} %bitcast.2, bf16[64,8192]{1,0:T(8,128)(2,1)} %q_hbm.1, bf16[64,8192]{1,0:T(8,128)(2,1)} %do_hbm.1, ...), custom_call_target="tpu_custom_call" | custom-call | tf_op jit(solution)/shard_map/pallas_call | solution.py:466
  54.3 1.6 %shard_map.102 = (bf16[64,8192]{1,0:T(8,128)(2,1)}, bf16[64,8192]{1,0:T(8,128)(2,1)}, bf16[64,1024]{1,0:T(8,128)(2,1)}, bf16[64,1024]{1,0:T(8,128)(2,1)}, f32[8,512]{1,0:T(8,128)}) custom-call(bf16[8,64,1024]{2,1,0:T(8,128)(2,1)S(1)} %get-tuple-element.15.outs, bf16[8,64,1024]{2,1,0:T(8,128)(2,1)S(1)} %get-tuple-element.16.dqs, ...), custom_call_target="tpu_custom_call" | custom-call | tf_op jit(solution)/shard_map/pallas_call | solution.py:506

commit v4 on v3

--- a/solution.py
+++ b/solution.py
@@ -22,6 +22,8 @@
 PER = 4
 SPLIT = 6
 SPLIT_ROWS = 3
+FAR = (4, 3, 5, 2, 6, 1, 7)
+NEXT = (7, 6, 5, 4, 3, 2, 1)
 VMEM_LIMIT = 40 << 20
 
 
@@ -47,7 +49,7 @@
         )
     pl.semaphore_signal(barrier, inc=1, device_id=above, device_id_type=MESH)
     pl.semaphore_signal(barrier, inc=1, device_id=below, device_id_type=MESH)
-    pl.semaphore_wait(barrier, HEADS + 1)
+    return barrier
 
 
 def remote(src, dst, send, recv, device):
@@ -67,6 +69,7 @@
 ):
     me, half, j, own, cycle, above, below = place()
     ins, keep, grads = (k_ref, v_ref), (kk, vv), (gk, gv)
+    barrier = greet(me, above, below)
     width = HEADS * D
     loads = []
     facts = [
@@ -79,8 +82,6 @@
         cols = pl.ds(h * width, width)
         loads.append(pltpu.make_async_copy(q_hbm.at[:, cols], qs.at[h], q_sem.at[0, h]))
         loads.append(pltpu.make_async_copy(do_hbm.at[:, cols], dos.at[h], q_sem.at[1, h]))
-    for copy in loads:
-        copy.start()
 
     def each(action):
         for p in range(HEADS):
@@ -88,6 +89,18 @@
             def _(p=p):
                 action(p)
 
+    def around(order, action):
+        for step in order:
+            action(lax.rem(me + step, HEADS))
+
+    def around_sized(order, action):
+        for step in order:
+            p = lax.rem(me + step, HEADS)
+            for jj in range(STEPS):
+                @pl.when(lax.rem(p, STEPS) == jj)
+                def _(p=p, jj=jj):
+                    action(p, jj)
+
     def branch(action):
         for jj in range(STEPS):
             @pl.when(j == jj)
@@ -100,9 +113,12 @@
             def _(jj=jj):
                 action(jj)
 
+    def lanes_of(p):
+        return pl.ds(p * D if isinstance(p, int) else pl.multiple_of(p * D, D), D)
+
     def spread(p, kv, src):
         return remote(
-            ins[kv].at[:, pl.ds(p * D, D)], hb.at[kv, pl.ds(src * ROWS, ROWS)],
+            ins[kv].at[:, lanes_of(p)], hb.at[kv, pl.ds(src * ROWS, ROWS)],
             s1_send.at[p, kv], s1_recv.at[src, kv], {"head": p},
         )
 
@@ -160,7 +176,7 @@
 
     def give_back(p, kv, src):
         return remote(
-            tsel.at[p // STEPS, kv, pl.ds((p % STEPS) * ROWS, ROWS)],
+            tsel.at[p // STEPS, kv, pl.ds(lax.rem(p, STEPS) * ROWS, ROWS)],
             xb.at[kv, :, pl.ds(src * D, D)],
             t1_send.at[p, kv], t1_recv.at[src, kv], {"head": p},
         )
@@ -168,9 +184,9 @@
     def entropy_to(p, src):
         return remote(es.at[p], eb.at[src], e_send.at[p], e_recv.at[src], {"head": p})
 
-    greet(me, above, below)
+    pl.semaphore_wait(barrier, HEADS + 1)
     for kv in range(2):
-        each(lambda p: spread(p, kv, me).start())
+        around(FAR, lambda p: spread(p, kv, me).start())
     mine = [
         pltpu.make_async_copy(
             ins[kv].at[:, pl.ds(me * D, D)], hb.at[kv, pl.ds(me * ROWS, ROWS)], local.at[kv]
@@ -182,7 +198,7 @@
         )
         for kv in range(2)
     ]
-    for copy in mine:
+    for copy in mine + loads:
         copy.start()
 
     for copy in facts:

time: 56 us -> 55.9 us (level)
  no operation moved by 1% of the time
where the time goes in v4:
time: 55.9 us; the launch traced here: 55.8 us
  Pallas kernels  55.1 us (99%)
  between operations  0.64 us (1%)
    pallas_call x1, Pallas kernels, body(): pl.pallas_call(kernel, out_shape=(stacked, stacked, grad, grad, entropy),...  53.6 us
    pallas_call x1, Pallas kernels, body(): pl.pallas_call(write_kernel, out_shape=(tokens, tokens, grad, grad, entro...  1.56 us

profile of v4, /device:TPU:1, one launch (start us, length us, event | category | flops | bytes accessed | tf_op | source)
XLA Modules:
  0.0 55.8 jit_solution(117159471308932363)
XLA Ops:
  0.6 53.6 %shard_map.101 = (bf16[8,64,1024]{2,1,0:T(8,128)(2,1)S(1)}, bf16[8,64,1024]{2,1,0:T(8,128)(2,1)S(1)}, bf16[64,1024]{1,0:T(8,128)(2,1)S(1)}, bf16[64,1024]{1,0:T(8,128)(2,1)S(1)}, f32[8,512]{1,0:T(8,128)S(1)}) custom-call(s32[64]{0:T(128)} %order_hbm.1, s32[1,128]{1,0:T(1,128)} %bitcast.2, bf16[64,8192]{1,0:T(8,128)(2,1)} %q_hbm.1, bf16[64,8192]{1,0:T(8,128)(2,1)} %do_hbm.1, ...), custom_call_target="tpu_custom_call" | custom-call | tf_op jit(solution)/shard_map/pallas_call | solution.py:482
  54.2 1.6 %shard_map.102 = (bf16[64,8192]{1,0:T(8,128)(2,1)}, bf16[64,8192]{1,0:T(8,128)(2,1)}, bf16[64,1024]{1,0:T(8,128)(2,1)}, bf16[64,1024]{1,0:T(8,128)(2,1)}, f32[8,512]{1,0:T(8,128)}) custom-call(bf16[8,64,1024]{2,1,0:T(8,128)(2,1)S(1)} %get-tuple-element.15.outs, bf16[8,64,1024]{2,1,0:T(8,128)(2,1)S(1)} %get-tuple-element.16.dqs, ...), custom_call_target="tpu_custom_call" | custom-call | tf_op jit(solution)/shard_map/pallas_call | solution.py:522
